TPU v7x, 128 devices: a whole 4x4x4 slice. The times are simulated.
128 devices in a mesh: particle: 16 (over y_hi, z, core), slab: 8 (over x, y_lo).
Axes of the slice: x: 4, y: 4 (y_hi: 2, y_lo: 2; y = y_hi * 2 + y_lo), z: 4, core: 2. Of those that a mesh axis runs over, the one named last changes fastest.
Arguments:
- latent: float32 [32, 16, 128, 128], P('particle', None, 'slab'), may hold values from -6 to 6
- ancestors: int32 [4, 32], replicated, may hold values from 0 to 31
- noise: float32 [4, 32, 16, 128, 128], P(None, 'particle', None, 'slab'), may hold values from -6 to 6
- embed_weight: bfloat16 [16, 256], replicated, may hold values from -1.5 to 1.5
- depth_weight: bfloat16 [7, 7, 256], replicated, may hold values from -0.875 to 0.875
- depth_bias: float32 [256], replicated, may hold values from -3 to 3
- norm_gain: float32 [256], replicated, may hold values from 0.5 to 2
- norm_shift: float32 [256], replicated, may hold values from -3 to 3
- inner_weight: bfloat16 [256, 1024], replicated, may hold values from -0.375 to 0.375
- inner_bias: float32 [1024], replicated, may hold values from -3 to 3
- outer_weight: bfloat16 [1024, 256], replicated, may hold values from -0.1875 to 0.1875
- outer_bias: float32 [256], replicated, may hold values from -3 to 3
- head_weight: bfloat16 [256, 16], replicated, may hold values from -0.375 to 0.375
Outputs:
- final_latent: float32 [32, 16, 128, 128], P('particle', None, 'slab')
All inputs are finite; a program needn't handle non-finite values.
Results may differ from a plain program's by a relative error of at most 0.0095.
Values may be sent and summed in bfloat16 or wider, within the bound.
No kernel may reach another device: no remote copies, remote signals or barrier semaphores. Data moves between devices by JAX's collectives and lax.ppermute only.
A program may use at most 64 MiB of HBM per device.

v0:
```python
import jax
import jax.numpy as jnp
from jax import lax
from jax.sharding import PartitionSpec as P

STEPS = 4


def extended(cells, sides, width):
    for axis, dim in sides:
        count = lax.axis_size(axis)
        ends = count - 1
        head = lax.slice_in_dim(cells, 0, width, axis=dim)
        tail = lax.slice_in_dim(cells, cells.shape[dim] - width, cells.shape[dim], axis=dim)
        cells = jnp.concatenate(
            [
                lax.ppermute(tail, axis, [(i, (i + 1) % count) for i in range(ends)]),
                cells,
                lax.ppermute(head, axis, [((i + 1) % count, i) for i in range(ends)]),
            ],
            axis=dim,
        )
    return cells


def embed_latent(source, embed_weight):
    return jnp.einsum(
        "pcrw,cd->prwd",
        source.astype(jnp.bfloat16),
        embed_weight,
        preferred_element_type=jnp.float32,
    ).astype(jnp.bfloat16)


def network(
    latent,
    embed_weight,
    depth_weight,
    depth_bias,
    norm_gain,
    norm_shift,
    inner_weight,
    inner_bias,
    outer_weight,
    outer_bias,
    head_weight,
):
    count, channels, rows, width = latent.shape
    widened = extended(latent.astype(jnp.bfloat16), (("slab", 2),), 3).astype(latent.dtype)
    features_wide = embed_latent(widened, embed_weight)
    features = features_wide[:, 3 : 3 + rows]
    padded = jnp.pad(features_wide, ((0, 0), (0, 0), (3, 3), (0, 0)))
    total = jnp.zeros(features.shape, jnp.float32)
    for row_off in range(7):
        for col_off in range(7):
            total = total + padded[:, row_off : row_off + rows, col_off : col_off + width].astype(
                jnp.float32
            ) * depth_weight[row_off, col_off].astype(jnp.float32)
    conv = total + depth_bias
    center = jnp.mean(conv, axis=-1, keepdims=True)
    spread = jnp.mean((conv - center) ** 2, axis=-1, keepdims=True)
    normed = ((conv - center) * lax.rsqrt(spread + 1e-06) * norm_gain + norm_shift).astype(
        jnp.bfloat16
    )
    flat = normed.reshape(count * rows * width, -1)
    hidden = jax.nn.gelu(
        jnp.dot(flat, inner_weight, preferred_element_type=jnp.float32) + inner_bias
    ).astype(jnp.bfloat16)
    mixed = jnp.dot(hidden, outer_weight, preferred_element_type=jnp.float32) + outer_bias
    block = (features.reshape(count * rows * width, -1).astype(jnp.float32) + mixed).astype(
        jnp.bfloat16
    )
    block = block.reshape(count, rows, width, -1)
    return jnp.einsum("prwd,dc->pcrw", block, head_weight, preferred_element_type=jnp.float32)


def resample(moved, section_parents):
    count = moved.shape[0]
    own_index = lax.axis_index("particle")
    groups = lax.axis_size("particle")
    table = section_parents.reshape(groups, count)
    mine = own_index * count + jnp.arange(count, dtype=jnp.int32)
    selector = (table[:, :, None] == mine[None, None, :]).astype(jnp.float32)
    outgoing = jnp.einsum("djk,kcrw->djcrw", selector, moved, precision=lax.Precision.HIGHEST)
    received = lax.all_to_all(
        outgoing.astype(jnp.bfloat16), "particle", split_axis=0, concat_axis=0, tiled=True
    ).astype(outgoing.dtype)
    return jnp.sum(received, axis=0)


def per_device(
    latent,
    ancestors,
    noise,
    embed_weight,
    depth_weight,
    depth_bias,
    norm_gain,
    norm_shift,
    inner_weight,
    inner_bias,
    outer_weight,
    outer_bias,
    head_weight,
):
    state = latent
    for section in range(STEPS):
        predicted = network(
            state,
            embed_weight,
            depth_weight,
            depth_bias,
            norm_gain,
            norm_shift,
            inner_weight,
            inner_bias,
            outer_weight,
            outer_bias,
            head_weight,
        )
        moved = (0.9 - 0.05 * section) * state + 0.6 * predicted + 0.3 * noise[section]
        state = resample(moved, ancestors[section])
    return state


def solution(mesh):
    in_specs = (
        P("particle", None, "slab", None),
        P(),
        P(None, "particle", None, "slab", None),
        P(),
        P(),
        P(),
        P(),
        P(),
        P(),
        P(),
        P(),
        P(),
        P(),
    )
    out_specs = P("particle", None, "slab", None)
    return jax.shard_map(
        per_device, mesh=mesh, in_specs=in_specs, out_specs=out_specs, check_vma=False
    )
```

profile of v0, /device:TPU:2, one launch (start us, length us, event | category | flops | bytes accessed | tf_op | source)
XLA Modules:
  0.0 411.7 jit_solution(10593314584702425490)
XLA Ops:
  1.1 3.5 collective-permute-start
  4.6 3.3 collective-permute-start.1
  20.3 2.5 slice_convert_fusion.3
  23.2 34.7 %fusion.131 = (f32[2,16,128]{2,1,0:T(8,128)S(1)}, f32[2,16,128,256]{3,2,1,0:T(8,128)S(1)}) fusion(f32[256]{0:T(256)} %param.18, f32[256]{0:T(256)} %bitcast.371, f32[256]{0:T(256)} %bitcast.375, f32[256]{0:T(256)S(1)} %bitcast.187, f32[256]{0:T(256)S(1)} %bitcast.191, bf16[2,22,128,256]{3,2,1,0:T(8,128)(2,1)S(1)} %convolution_convert_fusion.3, ...), kind=kLoop, calls=%fused_computation.253 | loop fusion | flops 155185152 | bytes 21825536 | tf_op jit(solution)/shard_map/reduce_sum | solution.py:60
  60.7 9.6 %fusion.39 = bf16[4096,256]{1,0:T(8,128)(2,1)} fusion(f32[4096,256]{1,0:T(8,128)} %bitcast.171, bf16[1024,256]{1,0:T(8,128)(2,1)S(1)} %copy-done, bf16[4096,256]{1,0:T(8,128)(2,1)S(1)} %bitcast.176, bf16[256,1024]{1,0:T(8,128)(2,1)} %param.21, f32[1024]{0:T(1024)S(1)} %copy-done.80, f32[256]{0:T(256)S(1)} %copy-done.84), kind=kOutput, calls=%fused_computation.47 | convolution fusion | flops 4340056064 | bytes 9442304 | tf_op jit(solution)/shard_map/dot_general | solution.py:69
  75.6 37.0 %all_to_all.20 = bf16[16,2,16,16,128]{4,3,2,1,0:T(8,128)(2,1)S(1)} all-to-all(bf16[16,2,16,16,128]{4,3,2,1,0:T(8,128)(2,1)S(1)} %copy.50), channel_id=1, replica_groups=mesh['particle'=16,'slab'=8] {'particle'}, dimensions={0} | all-to-all | bytes 4194304 | tf_op jit(solution)/shard_map/all_to_all | solution.py:85
  115.0 4.8 %collective-permute-start.3 = (bf16[2,16,3,128]{3,1,2,0:T(8,128)(2,1)S(1)}, bf16[2,16,3,128]{3,1,2,0:T(8,128)(2,1)}, u32[]{:S(2)}, u32[]{:S(2)}) collective-permute-start(bf16[2,16,3,128]{3,1,2,0:T(8,128)(2,1)S(1)} %get-tuple-element.26), channel_id=1, source_target_pairs={{1,0},{2,1},{3,2},{4,3},{5,4},{6,5},{7,6},{9,8},{10,9},{11,10},{12... | collective-permute-start | bytes 73736 | tf_op jit(solution)/shard_map/ppermute | solution.py:19
  123.4 36.3 %fusion.130 = (f32[2,16,128]{2,1,0:T(8,128)S(1)}, f32[2,16,128,256]{3,2,1,0:T(8,128)S(1)}) fusion(f32[256]{0:T(256)} %param.18, f32[256]{0:T(256)} %bitcast.372, f32[256]{0:T(256)} %bitcast.376, f32[256]{0:T(256)} %bitcast.188, f32[256]{0:T(256)} %bitcast.192, bf16[2,22,128,256]{3,2,1,0:T(8,128)(2,1)S(1)} %convolution_convert_fusion.2, f32[256]{0:T(256)} %bitcast.196, ...), kind=kLoop, calls=%fused_computation.252 | loop fusion | flops 155185152 | bytes 21825536 | tf_op jit(solution)/shard_map/reduce_sum | solution.py:60
  159.8 2.5 slice_convert_fusion.2
  165.0 9.6 %fusion.38 = bf16[4096,256]{1,0:T(8,128)(2,1)} fusion(f32[4096,256]{1,0:T(8,128)} %bitcast.172, bf16[1024,256]{1,0:T(8,128)(2,1)S(1)} %copy-done, bf16[4096,256]{1,0:T(8,128)(2,1)S(1)} %bitcast.177, bf16[256,1024]{1,0:T(8,128)(2,1)} %param.21, f32[1024]{0:T(1024)S(1)} %copy-done.81, f32[256]{0:T(256)S(1)} %copy-done.85), kind=kOutput, calls=%fused_computation.46 | convolution fusion | flops 4340056064 | bytes 9442304 | tf_op jit(solution)/shard_map/dot_general | solution.py:69
  176.9 2.4 convolution_convert_fusion.6
  179.8 31.8 %all_to_all.21 = bf16[16,2,16,16,128]{4,3,2,1,0:T(8,128)(2,1)S(1)} all-to-all(bf16[16,2,16,16,128]{4,3,2,1,0:T(8,128)(2,1)S(1)} %copy.56), channel_id=1, replica_groups=mesh['particle'=16,'slab'=8] {'particle'}, dimensions={0} | all-to-all | bytes 4194304 | tf_op jit(solution)/shard_map/all_to_all | solution.py:85
  212.1 4.8 %collective-permute-start.4 = (bf16[2,16,3,128]{3,1,2,0:T(8,128)(2,1)S(1)}, bf16[2,16,3,128]{3,1,2,0:T(8,128)(2,1)S(1)}, u32[]{:S(2)}, u32[]{:S(2)}) collective-permute-start(bf16[2,16,3,128]{3,1,2,0:T(8,128)(2,1)S(1)} %get-tuple-element.23), channel_id=1, source_target_pairs={{0,1},{1,2},{2,3},{3,4},{4,5},{5,6},{6,7},{8,9},{9,10},{10,11},{11... | collective-permute-start | bytes 73736 | tf_op jit(solution)/shard_map/ppermute | solution.py:17
  220.2 2.6 collective-permute-done.5
  224.5 36.1 %fusion.129 = (f32[2,16,128]{2,1,0:T(8,128)S(1)}, f32[2,16,128,256]{3,2,1,0:T(8,128)S(1)}) fusion(f32[256]{0:T(256)} %param.18, f32[256]{0:T(256)} %bitcast.373, f32[256]{0:T(256)} %bitcast.377, f32[256]{0:T(256)} %bitcast.189, f32[256]{0:T(256)} %bitcast.193, bf16[2,22,128,256]{3,2,1,0:T(8,128)(2,1)S(1)} %convolution_convert_fusion.1, f32[256]{0:T(256)} %bitcast.197, ...), kind=kLoop, calls=%fused_computation.251 | loop fusion | flops 155185152 | bytes 21825536 | tf_op jit(solution)/shard_map/reduce_sum | solution.py:60
  260.6 2.5 slice_convert_fusion.1
  265.8 9.6 %fusion.37 = bf16[4096,256]{1,0:T(8,128)(2,1)} fusion(f32[4096,256]{1,0:T(8,128)} %bitcast.173, bf16[1024,256]{1,0:T(8,128)(2,1)S(1)} %copy-done, bf16[4096,256]{1,0:T(8,128)(2,1)S(1)} %bitcast.179, bf16[256,1024]{1,0:T(8,128)(2,1)} %param.21, f32[1024]{0:T(1024)S(1)} %copy-done.82, f32[256]{0:T(256)S(1)} %copy-done.86), kind=kOutput, calls=%fused_computation.45 | convolution fusion | flops 4340056064 | bytes 9442304 | tf_op jit(solution)/shard_map/dot_general | solution.py:69
  280.6 32.3 %all_to_all.22 = bf16[16,2,16,16,128]{4,3,2,1,0:T(8,128)(2,1)S(1)} all-to-all(bf16[16,2,16,16,128]{4,3,2,1,0:T(8,128)(2,1)S(1)} %copy.62), channel_id=1, replica_groups=mesh['particle'=16,'slab'=8] {'particle'}, dimensions={0} | all-to-all | bytes 4194304 | tf_op jit(solution)/shard_map/all_to_all | solution.py:85
  315.7 4.4 %collective-permute-start.7 = (bf16[2,16,3,128]{3,1,2,0:T(8,128)(2,1)S(1)}, bf16[2,16,3,128]{3,1,2,0:T(8,128)(2,1)}, u32[]{:S(2)}, u32[]{:S(2)}) collective-permute-start(bf16[2,16,3,128]{3,1,2,0:T(8,128)(2,1)S(1)} %get-tuple-element.22), channel_id=1, source_target_pairs={{1,0},{2,1},{3,2},{4,3},{5,4},{6,5},{7,6},{9,8},{10,9},{11,10},{12... | collective-permute-start | bytes 73736 | tf_op jit(solution)/shard_map/ppermute | solution.py:19
  323.5 36.2 %fusion.128 = (f32[2,16,128]{2,1,0:T(8,128)S(1)}, f32[2,16,128,256]{3,2,1,0:T(8,128)S(1)}) fusion(f32[256]{0:T(256)} %param.18, f32[256]{0:T(256)} %bitcast.374, f32[256]{0:T(256)} %bitcast.378, f32[256]{0:T(256)} %bitcast.190, f32[256]{0:T(256)} %bitcast.194, bf16[2,22,128,256]{3,2,1,0:T(8,128)(2,1)S(1)} %convolution_convert_fusion, f32[256]{0:T(256)} %bitcast.198, ...), kind=kLoop, calls=%fused_computation.250 | loop fusion | flops 155185152 | bytes 21825536 | tf_op jit(solution)/shard_map/reduce_sum | solution.py:60
  359.7 2.5 slice_convert_fusion
  365.9 9.0 %fusion.36 = bf16[4096,256]{1,0:T(8,128)(2,1)S(1)} fusion(f32[4096,256]{1,0:T(8,128)} %bitcast.174, bf16[1024,256]{1,0:T(8,128)(2,1)S(1)} %copy-done, bf16[4096,256]{1,0:T(8,128)(2,1)} %bitcast.181, bf16[256,1024]{1,0:T(8,128)(2,1)} %param.21, f32[1024]{0:T(1024)S(1)} %copy-done.83, f32[256]{0:T(256)S(1)} %copy-done.87), kind=kOutput, calls=%fused_computation.44 | convolution fusion | flops 4340056064 | bytes 9442304 | tf_op jit(solution)/shard_map/dot_general | solution.py:69
  375.5 2.4 convolution_convert_fusion.4
  378.4 32.1 %all_to_all.23 = bf16[16,2,16,16,128]{4,3,2,1,0:T(8,128)(2,1)S(1)} all-to-all(bf16[16,2,16,16,128]{4,3,2,1,0:T(8,128)(2,1)S(1)} %copy.68), channel_id=1, replica_groups=mesh['particle'=16,'slab'=8] {'particle'}, dimensions={0} | all-to-all | bytes 4194304 | tf_op jit(solution)/shard_map/all_to_all | solution.py:85
  (242 shorter events, 57.4 us)
Async XLA Ops:
  0.0 60.7 %copy-start = (bf16[1024,256]{1,0:T(8,128)(2,1)S(1)}, bf16[1024,256]{1,0:T(8,128)(2,1)}, u32[]{:S(2)}) copy-start(bf16[1024,256]{1,0:T(8,128)(2,1)} %param.23) | copy-start | bytes 1572868
  1.1 16.9 %collective-permute-start = (bf16[2,16,3,128]{3,1,2,0:T(8,128)(2,1)S(1)}, bf16[2,16,3,128]{3,1,2,0:T(8,128)(2,1)S(1)}, u32[]{:S(2)}, u32[]{:S(2)}) collective-permute-start(bf16[2,16,3,128]{3,1,2,0:T(8,128)(2,1)S(1)} %get-tuple-element.27), channel_id=1, source_target_pairs={{0,1},{1,2},{2,3},{3,4},{4,5},{5,6},{6,7},{8,9},{9,10},{10,11},{11... | collective-permute-start | bytes 73736 | tf_op jit(solution)/shard_map/ppermute | solution.py:17
  4.6 14.0 %collective-permute-start.1 = (bf16[2,16,3,128]{3,1,2,0:T(8,128)(2,1)S(1)}, bf16[2,16,3,128]{3,1,2,0:T(8,128)(2,1)}, u32[]{:S(2)}, u32[]{:S(2)}) collective-permute-start(bf16[2,16,3,128]{3,1,2,0:T(8,128)(2,1)S(1)} %get-tuple-element.28), channel_id=1, source_target_pairs={{1,0},{2,1},{3,2},{4,3},{5,4},{6,5},{7,6},{9,8},{10,9},{11,10},{12... | collective-permute-start | bytes 73736 | tf_op jit(solution)/shard_map/ppermute | solution.py:19
  9.5 13.4 %copy-start.14 = (f32[1,1,256]{2,1,0:T(1,128)}, f32[1,1,256]{2,1,0:T(1,128)S(1)}, u32[]{:S(2)}) copy-start(f32[1,1,256]{2,1,0:T(1,128)S(1)} %get-tuple-element.29) | copy-start | bytes 3076
  9.5 13.4 %copy-start.15 = (f32[1,1,256]{2,1,0:T(1,128)}, f32[1,1,256]{2,1,0:T(1,128)S(1)}, u32[]{:S(2)}) copy-start(f32[1,1,256]{2,1,0:T(1,128)S(1)} %get-tuple-element.30) | copy-start | bytes 3076
  9.5 13.3 %copy-start.16 = (f32[1,1,256]{2,1,0:T(1,128)}, f32[1,1,256]{2,1,0:T(1,128)S(1)}, u32[]{:S(2)}) copy-start(f32[1,1,256]{2,1,0:T(1,128)S(1)} %get-tuple-element.31) | copy-start | bytes 3076
  9.5 13.3 %copy-start.17 = (f32[1,1,256]{2,1,0:T(1,128)}, f32[1,1,256]{2,1,0:T(1,128)S(1)}, u32[]{:S(2)}) copy-start(f32[1,1,256]{2,1,0:T(1,128)S(1)} %get-tuple-element.32) | copy-start | bytes 3076
  60.7 9.7 %copy-start.7 = (f32[2,16,16,128]{3,2,1,0:T(8,128)S(1)}, f32[2,16,16,128]{3,2,1,0:T(8,128)}, u32[]{:S(2)}) copy-start(f32[2,16,16,128]{3,2,1,0:T(8,128)} %param.13) | copy-start | bytes 786436
  60.7 11.9 %copy-start.69 = (s32[2]{0:T(128)S(1)}, s32[2]{0:T(128)}, u32[]{:S(2)}) copy-start(s32[2]{0:T(128)} %iota_add_fusion) | copy-start | bytes 28
  60.7 11.9 %copy-start.74 = (s32[16,2]{0,1:T(2,128)S(1)}, s32[16,2]{0,1:T(2,128)}, u32[]{:S(2)}) copy-start(s32[16,2]{0,1:T(2,128)} %copy.45) | copy-start | bytes 388
  75.6 44.2 %copy-start.79 = (s32[32]{0:T(128)S(1)}, s32[32]{0:T(128)}, u32[]{:S(2)}) copy-start(s32[32]{0:T(128)} %get-tuple-element.8) | copy-start | bytes 388
  75.6 46.1 %copy-start.12 = (bf16[16,256]{1,0:T(8,128)(2,1)S(1)}, bf16[16,256]{1,0:T(8,128)(2,1)}, u32[]{:S(2)}) copy-start(bf16[16,256]{1,0:T(8,128)(2,1)} %param.16) | copy-start | bytes 24580
  113.0 7.5 %collective-permute-start.2 = (bf16[2,16,3,128]{3,1,2,0:T(8,128)(2,1)S(1)}, bf16[2,16,3,128]{3,1,2,0:T(8,128)(2,1)S(1)}, u32[]{:S(2)}, u32[]{:S(2)}) collective-permute-start(bf16[2,16,3,128]{3,1,2,0:T(8,128)(2,1)S(1)} %get-tuple-element.25), channel_id=1, source_target_pairs={{0,1},{1,2},{2,3},{3,4},{4,5},{5,6},{6,7},{8,9},{9,10},{10,11},{11... | collective-permute-start | bytes 73736 | tf_op jit(solution)/shard_map/ppermute | solution.py:17
  115.0 6.7 %collective-permute-start.3 = (bf16[2,16,3,128]{3,1,2,0:T(8,128)(2,1)S(1)}, bf16[2,16,3,128]{3,1,2,0:T(8,128)(2,1)}, u32[]{:S(2)}, u32[]{:S(2)}) collective-permute-start(bf16[2,16,3,128]{3,1,2,0:T(8,128)(2,1)S(1)} %get-tuple-element.26), channel_id=1, source_target_pairs={{1,0},{2,1},{3,2},{4,3},{5,4},{6,5},{7,6},{9,8},{10,9},{11,10},{12... | collective-permute-start | bytes 73736 | tf_op jit(solution)/shard_map/ppermute | solution.py:19
  165.0 11.9 %copy-start.70 = (s32[2]{0:T(128)S(1)}, s32[2]{0:T(128)}, u32[]{:S(2)}) copy-start(s32[2]{0:T(128)} %iota_add_fusion) | copy-start | bytes 28
  165.0 11.9 %copy-start.75 = (s32[16,2]{0,1:T(2,128)S(1)}, s32[16,2]{0,1:T(2,128)}, u32[]{:S(2)}) copy-start(s32[16,2]{0,1:T(2,128)} %copy.44) | copy-start | bytes 388
  179.8 39.0 %copy-start.78 = (s32[32]{0:T(128)S(1)}, s32[32]{0:T(128)}, u32[]{:S(2)}) copy-start(s32[32]{0:T(128)} %get-tuple-element.6) | copy-start | bytes 388
  212.1 7.5 %collective-permute-start.4 = (bf16[2,16,3,128]{3,1,2,0:T(8,128)(2,1)S(1)}, bf16[2,16,3,128]{3,1,2,0:T(8,128)(2,1)S(1)}, u32[]{:S(2)}, u32[]{:S(2)}) collective-permute-start(bf16[2,16,3,128]{3,1,2,0:T(8,128)(2,1)S(1)} %get-tuple-element.23), channel_id=1, source_target_pairs={{0,1},{1,2},{2,3},{3,4},{4,5},{5,6},{6,7},{8,9},{9,10},{10,11},{11... | collective-permute-start | bytes 73736 | tf_op jit(solution)/shard_map/ppermute | solution.py:17
  216.9 5.8 %collective-permute-start.5 = (bf16[2,16,3,128]{3,1,2,0:T(8,128)(2,1)S(1)}, bf16[2,16,3,128]{3,1,2,0:T(8,128)(2,1)}, u32[]{:S(2)}, u32[]{:S(2)}) collective-permute-start(bf16[2,16,3,128]{3,1,2,0:T(8,128)(2,1)S(1)} %get-tuple-element.24), channel_id=1, source_target_pairs={{1,0},{2,1},{3,2},{4,3},{5,4},{6,5},{7,6},{9,8},{10,9},{11,10},{12... | collective-permute-start | bytes 73736 | tf_op jit(solution)/shard_map/ppermute | solution.py:19
  265.8 11.9 %copy-start.71 = (s32[2]{0:T(128)S(1)}, s32[2]{0:T(128)}, u32[]{:S(2)}) copy-start(s32[2]{0:T(128)} %iota_add_fusion) | copy-start | bytes 28
  265.8 11.9 %copy-start.76 = (s32[16,2]{0,1:T(2,128)S(1)}, s32[16,2]{0,1:T(2,128)}, u32[]{:S(2)}) copy-start(s32[16,2]{0,1:T(2,128)} %copy.43) | copy-start | bytes 388
  280.6 39.5 %copy-start.77 = (s32[32]{0:T(128)S(1)}, s32[32]{0:T(128)}, u32[]{:S(2)}) copy-start(s32[32]{0:T(128)} %get-tuple-element.5) | copy-start | bytes 388
  313.4 7.5 %collective-permute-start.6 = (bf16[2,16,3,128]{3,1,2,0:T(8,128)(2,1)S(1)}, bf16[2,16,3,128]{3,1,2,0:T(8,128)(2,1)S(1)}, u32[]{:S(2)}, u32[]{:S(2)}) collective-permute-start(bf16[2,16,3,128]{3,1,2,0:T(8,128)(2,1)S(1)} %get-tuple-element.21), channel_id=1, source_target_pairs={{0,1},{1,2},{2,3},{3,4},{4,5},{5,6},{6,7},{8,9},{9,10},{10,11},{11... | collective-permute-start | bytes 73736 | tf_op jit(solution)/shard_map/ppermute | solution.py:17
  315.7 6.1 %collective-permute-start.7 = (bf16[2,16,3,128]{3,1,2,0:T(8,128)(2,1)S(1)}, bf16[2,16,3,128]{3,1,2,0:T(8,128)(2,1)}, u32[]{:S(2)}, u32[]{:S(2)}) collective-permute-start(bf16[2,16,3,128]{3,1,2,0:T(8,128)(2,1)S(1)} %get-tuple-element.22), channel_id=1, source_target_pairs={{1,0},{2,1},{3,2},{4,3},{5,4},{6,5},{7,6},{9,8},{10,9},{11,10},{12... | collective-permute-start | bytes 73736 | tf_op jit(solution)/shard_map/ppermute | solution.py:19
  (72 other events, 364.3 us)
where the time goes:
time: 417 us; the launch traced here: 412 us
  other arithmetic  172 us (41%)
  blocking collectives  133 us (32%)
  matrix products  61.5 us (15%)
  starting transfers between devices  27 us (6%)
  local copies, waits for them, and re-layouts  12.8 us (3%)
    reduce_sum x4, other arithmetic, network(): center = jnp.mean(conv, axis=-1, keepdims=True)  143 us
    all_to_all x4, blocking collectives, resample(): lax.all_to_all(outgoing.astype(jnp.bfloat16), 'particle', split_axis=0, c...  133 us
    dot_general x4, matrix products, network(): jnp.dot(hidden, outer_weight, preferred_element_type=jnp.float32)  37.9 us
    ppermute x4, starting transfers between devices, extended(): lax.ppermute(head, axis, [((i + 1) % count, i) for i in range(ends)])  14.4 us
    ppermute x4, starting transfers between devices, extended(): lax.ppermute(tail, axis, [(i, (i + 1) % count) for i in range(ends)])  12.5 us
    convert_element_type x4, other arithmetic, network(): features.reshape(count * rows * width, -1).astype(jnp.float32) + mixed  10.1 us
    dot_general x4, matrix products, resample(): jnp.einsum('djk,kcrw->djcrw', selector, moved, precision=lax.Precision.HI...  9.41 us
  transfers between devices with their start and end apart: 8, of which 3 were waited for; matrix products, arithmetic and copies ran while one was open for 3% of the time, Pallas kernels for 0%

commit v1 on v0

v1 whole, which is shorter than its diff:
```python
import functools

import jax
import jax.numpy as jnp
from jax import lax
from jax.experimental import pallas as pl
from jax.experimental.pallas import tpu as pltpu
from jax.sharding import PartitionSpec as P

STEPS = 4
BF = jnp.bfloat16
F32 = jnp.float32
CUBIC = 0.7978845608028654 * 0.044715
SCALE = CUBIC ** (-1.0 / 3.0)
LINEAR = 0.7978845608028654 * SCALE
SRC, PARTICLE, NUMBER = 0, 32, 64
VMEM = pl.BlockSpec(memory_space=pltpu.VMEM)
SMEM = pl.BlockSpec(memory_space=pltpu.SMEM)


def table_kernel(final_count, anc, place, tab, live, slot):
    steps, count = anc.shape
    first = place[1] * final_count

    def clear(q, carry):
        for s in range(steps):
            live[s, q] = 0
            tab[s, SRC + q] = 0
            tab[s, PARTICLE + q] = 0
        return carry

    lax.fori_loop(0, count, clear, 0)

    def mark_last(p, carry):
        live[steps - 1, anc[steps - 1, first + p]] = 1
        return carry

    lax.fori_loop(0, final_count, mark_last, 0)
    for s in range(steps - 2, -1, -1):

        def mark(q, carry, s=s):
            a = anc[s, q]
            live[s, a] = live[s, a] | live[s + 1, q]
            return carry

        lax.fori_loop(0, count, mark, 0)
    for s in range(steps):

        def fill(q, n, s=s):
            slot[s, q] = n
            tab[s, SRC + n] = n if s == 0 else slot[s - 1, anc[s - 1, q]]
            tab[s, PARTICLE + n] = q
            return n + live[s, q]

        tab[s, NUMBER] = lax.fori_loop(0, count, fill, jnp.int32(0))

    def final(p, carry):
        tab[steps, p] = slot[steps - 1, anc[steps - 1, first + p]]
        return carry

    lax.fori_loop(0, final_count, final, 0)


def make_table(ancestors, place, final_count):
    steps, count = ancestors.shape
    return pl.pallas_call(
        functools.partial(table_kernel, final_count),
        out_shape=jax.ShapeDtypeStruct((steps + 1, 128), jnp.int32),
        in_specs=[SMEM, SMEM],
        out_specs=SMEM,
        scratch_shapes=[pltpu.SMEM((steps, count), jnp.int32), pltpu.SMEM((steps, count), jnp.int32)],
        name="table",
    )(ancestors, place)


def shifted(row, off):
    width = row.shape[1]
    if off == 0:
        return row
    zeros = jnp.zeros((row.shape[0], abs(off)), row.dtype)
    if off > 0:
        return jnp.concatenate([row[:, off:], zeros], axis=1)
    return jnp.concatenate([zeros, row[:, : width + off]], axis=1)


def step_kernel(
    step,
    last,
    tab,
    place,
    own_f,
    own_b,
    part,
    side,
    other,
    noise,
    wconv,
    gain,
    shift,
    win,
    bin_,
    wout,
    wskip,
    moved_f,
    moved_b,
    *rest,
):
    low = place[0] == 0
    flip = place[2]
    ready = rest[-1]
    width = own_b.shape[3]
    chunk = 256

    def convolve(t):
        src = tab[step, SRC + t]
        p0, p1, far = part[src, 0], part[src, 1], other[src]
        s0, s1, s2 = side[src, 0], side[src, 1], side[src, 2]
        rows = [
            lax.select(low, s0, far),
            lax.select(low, s1, p0),
            lax.select(low, s2, p1),
            own_b[src, 0],
            own_b[src, 1],
            lax.select(low, p0, s1),
            lax.select(low, p1, s2),
            lax.select(low, far, s0),
        ]
        taps = [[shifted(row, off) for off in range(-3, 4)] for row in rows]
        ones = jnp.ones((16, width), BF)
        stacks = [jnp.concatenate(sum(taps[r : r + 7], []) + [ones], axis=0) for r in range(2)]
        conv = jnp.dot(wconv[...], jnp.concatenate(stacks, axis=1), preferred_element_type=F32)
        spread = jnp.mean(conv * conv, axis=0, keepdims=True)
        return (conv * lax.rsqrt(spread + 1e-06) * gain[...] + shift[...]).astype(BF)

    def finish(t, normed):
        src = tab[step, SRC + t]
        ones = jnp.ones((16, 2 * width), BF)
        center = jnp.concatenate([own_b[src, 0], own_b[src, 1]], axis=1)
        acc = jnp.dot(wskip[...], jnp.concatenate([center, ones], axis=0), preferred_element_type=F32)
        for h in range(0, win.shape[0], chunk):
            y = jnp.dot(win[h : h + chunk], normed, preferred_element_type=F32)
            y = (y + bin_[h : h + chunk]).astype(BF)
            gate = jnp.tanh(y * (y * y + BF(LINEAR))) + BF(1.0)
            acc = acc + jnp.dot(wout[:, h : h + chunk], y * gate, preferred_element_type=F32)
        q = tab[step, PARTICLE + t]
        source = (q // 2) ^ flip
        for r in range(2):
            value = (
                (0.9 - 0.05 * step) * own_f[src, r].astype(F32)
                + acc[:, r * width : (r + 1) * width]
                + 0.3 * noise[source, 1 + step, q % 2, r].astype(F32)
            )
            moved_f[t, r] = value
            moved_b[t, r] = value.astype(BF)

    def body(t, carry):
        normed = ready[...]
        following = convolve(t)
        finish(jnp.maximum(t - 1, 0), normed)
        ready[...] = following
        return carry

    lax.fori_loop(0, tab[step, NUMBER] + 1, body, 0)
    if last:
        final = rest[0]

        def emit(p, carry):
            final[p] = moved_b[tab[step + 1, p ^ (2 * flip)]]
            return carry

        lax.fori_loop(0, final.shape[0], emit, 0)


def run_step(step, last, *operands):
    own_b, wconv = operands[3], operands[8]
    outs = [jax.ShapeDtypeStruct(own_b.shape, F32), jax.ShapeDtypeStruct(own_b.shape, BF)]
    if last:
        outs.append(jax.ShapeDtypeStruct(own_b.shape, BF))
    return pl.pallas_call(
        functools.partial(step_kernel, step, last),
        out_shape=outs,
        in_specs=[SMEM, SMEM] + [VMEM] * (len(operands) - 2),
        out_specs=[VMEM] * len(outs),
        scratch_shapes=[pltpu.VMEM((wconv.shape[0], 2 * own_b.shape[3]), BF)],
        compiler_params=pltpu.CompilerParams(vmem_limit_bytes=40 << 20),
        cost_estimate=pl.CostEstimate(flops=4 << 30, bytes_accessed=4 << 20, transcendentals=0),
        name=f"step{step}",
    )(*operands)


def pack_kernel(tab, place, states, packed):
    def copy(i, carry):
        q = tab[0, PARTICLE + i]
        packed[i] = states[(q // 2) ^ place[2], 0, q % 2]
        return carry

    lax.fori_loop(0, packed.shape[0], copy, 0)


def pack(slots, tab, place, states):
    return pl.pallas_call(
        pack_kernel,
        out_shape=jax.ShapeDtypeStruct((slots,) + states.shape[3:], BF),
        in_specs=[SMEM, SMEM, VMEM],
        out_specs=VMEM,
        name="pack",
    )(tab, place, states)


def high_low(x):
    high = x.astype(BF)
    return high, (x - high.astype(F32)).astype(BF)


def weights(embed, depth, depth_bias, gain, shift, inner, inner_bias, outer, outer_bias, head, pos):
    hp = lax.Precision.HIGHEST
    full = depth.astype(F32)[:, :, None, :] * embed.astype(F32)[None, None]
    dim = full.shape[-1]
    full = full.reshape(-1, dim)
    full = full - jnp.mean(full, axis=-1, keepdims=True)
    bias = depth_bias - jnp.mean(depth_bias)
    bh, bl = high_low(bias)
    wconv = jnp.concatenate([full.astype(BF), bh[None], bl[None], jnp.zeros((14, dim), BF)], axis=0).T
    wide = lambda v, s: jnp.broadcast_to((v * s)[:, None], (v.shape[0], pos))
    head_f = head.astype(F32)
    wout = (jnp.dot(outer.astype(F32), head_f, precision=hp) * (0.3 * SCALE)).astype(BF).T
    wskip = 0.6 * jnp.dot(embed.astype(F32), head_f, precision=hp)
    oh, ol = high_low(0.6 * jnp.dot(outer_bias[None], head_f, precision=hp))
    wskip = jnp.concatenate([wskip.astype(BF), oh, ol, jnp.zeros((14, head.shape[1]), BF)], axis=0).T
    return (
        wconv,
        wide(gain, 1.0 / SCALE),
        wide(shift, 1.0 / SCALE),
        inner.T,
        wide(inner_bias, 1.0 / SCALE),
        wout,
        wskip,
    )


def per_device(latent, ancestors, noise, embed, depth, depth_bias, gain, shift, inner, inner_bias, outer, outer_bias, head):
    here, channels, rows, width = latent.shape
    parts, slabs = lax.axis_size("particle"), lax.axis_size("slab")
    both = ("particle", "slab")
    half = parts // 2
    chips = half // 2
    total = chips * slabs

    def spot(which, chip, core):
        slab, at = divmod(chip, chips)
        at = chips - 1 - at if slab % 2 else at
        return (which * half + 2 * at + core) * slabs + slab

    sides = [
        pair
        for h in range(2)
        for m in range(total - 1)
        for pair in ((spot(h, m, 0), spot(h, m + 1, 0)), (spot(h, m + 1, 1), spot(h, m, 1)))
    ]
    swapped = [(i, i ^ 1) for i in range(parts)]
    members = [
        [[spot(h, chips * k + m, c) for m in range(chips) for c in range(2)] for h in range(2)] for k in range(slabs)
    ]
    columns = [pair[0] + pair[1] for pair in members]
    halves = [group for pair in members for group in pair]

    at = lax.axis_index("particle")
    core = at % 2
    place = jnp.stack([core, at // half, (lax.axis_index("slab") % 2) * (half - 2)]).astype(jnp.int32)
    tab = make_table(ancestors, place, half * here)
    stacked = jnp.concatenate([latent[None].astype(BF), noise.astype(BF)], axis=0)
    each = rows // half
    stacked = stacked.reshape(STEPS + 1, here, channels, half, each, width).transpose(3, 0, 1, 4, 2, 5)
    outgoing = jnp.concatenate([stacked, stacked], axis=0).reshape(parts, -1, width)
    incoming = lax.all_to_all(outgoing, both, split_axis=0, concat_axis=0, axis_index_groups=columns, tiled=True)
    incoming = incoming.reshape(parts, STEPS + 1, here, each, channels, width)
    params = weights(embed, depth, depth_bias, gain, shift, inner, inner_bias, outer, outer_bias, head, each * width)
    own_f = own_b = pack(half * here, tab, place, incoming)
    for step in range(STEPS):
        part = lax.ppermute(own_b, "particle", swapped)
        near = lax.dynamic_slice_in_dim(own_b, 1 - core, 1, axis=1)
        side = lax.ppermute(jnp.concatenate([near, part], axis=1), both, sides)
        other = lax.ppermute(lax.dynamic_index_in_dim(side, 2 - core, axis=1, keepdims=False), "particle", swapped)
        outs = run_step(step, step == STEPS - 1, tab, place, own_f, own_b, part, side, other, incoming, *params)
        own_f, own_b = outs[0], outs[1]
    final = outs[2].reshape(half, -1, width)
    home = lax.all_to_all(final, both, split_axis=0, concat_axis=0, axis_index_groups=halves, tiled=True)
    home = home.reshape(half, here, each, channels, width).transpose(1, 3, 0, 2, 4)
    return home.reshape(here, channels, rows, width).astype(F32)


def solution(mesh):
    in_specs = (
        P("particle", None, "slab", None),
        P(),
        P(None, "particle", None, "slab", None),
    ) + (P(),) * 10
    out_specs = P("particle", None, "slab", None)
    return jax.shard_map(per_device, mesh=mesh, in_specs=in_specs, out_specs=out_specs, check_vma=False)
```

time: 417 us -> 134 us (0.32)
  other arithmetic: 172 us -> 7.2 us
  blocking collectives: 133 us -> 8.48 us
  matrix products: 61.5 us -> 1.19 us
  Pallas kernels: 0 us -> 45.4 us
  waiting for transfers between devices: 3.4 us -> 39.5 us
  starting transfers between devices: 27 us -> 16.9 us
    reduce_sum x12 -> x2, other arithmetic: 150 us -> 0.79 us  [the longest x1 0.6 us: weights(): bias = depth_bias - jnp.mean(depth_bias)]
    all_to_all x4 -> x1, blocking collectives: 133 us -> 8.48 us  [per_device(): lax.all_to_all(final, both, split_axis=0, concat_axis=0, axis_index_group...]
    dot_general x16 -> x3, matrix products: 61.5 us -> 1.19 us  [the longest x1 0.83 us: weights(): wskip = 0.6 * jnp.dot(embed.astype(F32), head_f, precision=hp)]
    pallas_call x0 -> x6, Pallas kernels: none -> 45.4 us  [the longest x4 38.1 us: run_step(): pl.pallas_call(functools.partial(step_kernel, step, last), out_shape=outs...]
    ppermute x8 -> x12, waiting for transfers between devices: 3.4 us -> 33.8 us  [the longest x4 26.1 us: per_device(): side = lax.ppermute(jnp.concatenate([near, part], axis=1), both, sides)]
    ppermute x8 -> x12, starting transfers between devices: 27 us -> 8.67 us  [the longest x4 7.68 us: per_device(): side = lax.ppermute(jnp.concatenate([near, part], axis=1), both, sides)]
    convert_element_type x11 -> x6, other arithmetic: 21 us -> 3.07 us  [the longest x1 1.3 us: per_device(): noise.astype(BF)]
    all_to_all x0 -> x1, starting transfers between devices: none -> 8.19 us  [per_device(): lax.all_to_all(outgoing, both, split_axis=0, concat_axis=0, axis_index_gr...]
  transfers between devices with their start and end apart: 8 -> 13, of which waited for: 3 -> 12; matrix products, arithmetic and copies ran while one was open for 3% -> 9% of each run, Pallas kernels for 0% -> 4%
where the time goes in v1:
time: 134 us; the launch traced here: 131 us
  Pallas kernels  45.4 us (34%)
  waiting for transfers between devices  39.5 us (29%)
  starting transfers between devices  16.9 us (13%)
  local copies, waits for them, and re-layouts  11.5 us (9%)
  blocking collectives  8.48 us (6%)
  other arithmetic  7.2 us (5%)
    pallas_call x4, Pallas kernels, run_step(): pl.pallas_call(functools.partial(step_kernel, step, last), out_shape=outs...  38.1 us
    ppermute x4, waiting for transfers between devices, per_device(): side = lax.ppermute(jnp.concatenate([near, part], axis=1), both, sides)  26.1 us
    all_to_all x1, blocking collectives, per_device(): lax.all_to_all(final, both, split_axis=0, concat_axis=0, axis_index_group...  8.48 us
    all_to_all x1, starting transfers between devices, per_device(): lax.all_to_all(outgoing, both, split_axis=0, concat_axis=0, axis_index_gr...  8.19 us
    ppermute x4, starting transfers between devices, per_device(): side = lax.ppermute(jnp.concatenate([near, part], axis=1), both, sides)  7.68 us
    all_to_all x1, waiting for transfers between devices, per_device(): lax.all_to_all(outgoing, both, split_axis=0, concat_axis=0, axis_index_gr...  5.69 us
    pallas_call x1, Pallas kernels, make_table(): pl.pallas_call(functools.partial(table_kernel, final_count), out_shape=ja...  5.06 us
    ppermute x4, waiting for transfers between devices, per_device(): part = lax.ppermute(own_b, 'particle', swapped)  3.96 us
  transfers between devices with their start and end apart: 13, of which 12 were waited for; matrix products, arithmetic and copies ran while one was open for 9% of the time, Pallas kernels for 4%

profile of v1, /device:TPU:2, one launch (start us, length us, event | category | flops | bytes accessed | tf_op | source)
XLA Modules:
  0.0 131.3 jit_solution(11801267606790212247)
XLA Ops:
  1.0 1.3 convert_element_type.64
  4.1 1.9 %copy.29 = bf16[16,5,2,2,16,128]{5,4,3,2,1,0:T(8,128)(2,1)} copy(bf16[16,5,2,2,16,128]{5,3,0,4,2,1:T(2,128)(2,1)S(1)} %pad_maximum_fusion) | data formatting | bytes 2621440 | tf_op jit(solution)/shard_map/concatenate | solution.py:274
  6.1 8.2 %all-to-all-start = ((bf16[16,320,128]{2,1,0:T(8,128)(2,1)}), bf16[16,320,128]{2,1,0:T(8,128)(2,1)S(1)}, u32[]{:S(2)}, u32[]{:S(2)}) async-start(bf16[16,320,128]{2,1,0:T(8,128)(2,1)} %bitcast.6), calls=%async_computation | async-start | bytes 2621440 | tf_op jit(solution)/shard_map/all_to_all | solution.py:275
  21.6 5.1 %table.1.tab = s32[5,128]{1,0:T(8,128)} custom-call(s32[4,32]{1,0:T(4,128)} %anc.1, s32[3]{0:T(128)} %pad_add_fusion.place), custom_call_target="tpu_custom_call" | custom-call | tf_op jit(solution)/shard_map/table/pallas_call | solution.py:66
  29.4 5.7 %all-to-all-done = bf16[16,320,128]{2,1,0:T(8,128)(2,1)S(1)} async-done(((bf16[16,320,128]{2,1,0:T(8,128)(2,1)}), bf16[16,320,128]{2,1,0:T(8,128)(2,1)S(1)}, u32[]{:S(2)}, u32[]{:S(2)}) %all-to-all-start) | async-done | bytes 1310752 | tf_op jit(solution)/shard_map/all_to_all | solution.py:275
  36.2 2.2 %pack.1.own_f.own_b = bf16[16,2,16,128]{3,2,1,0:T(8,128)(2,1)} custom-call(s32[5,128]{1,0:T(8,128)} %table.1.tab, s32[3]{0:T(128)} %pad_add_fusion.place, bf16[16,5,2,2,16,128]{5,4,3,2,1,0:T(8,128)(2,1)} %bitcast.46), custom_call_target="tpu_custom_call" | custom-call | tf_op jit(solution)/shard_map/pack/pallas_call | solution.py:201
  40.0 1.9 %collective-permute-start.1 = (bf16[16,3,16,128]{3,2,1,0:T(8,128)(2,1)S(1)}, bf16[16,3,16,128]{3,2,1,0:T(8,128)(2,1)S(1)}, u32[]{:S(2)}, u32[]{:S(2)}) collective-permute-start(bf16[16,3,16,128]{3,2,1,0:T(8,128)(2,1)S(1)} %pad_maximum_fusion.1), channel_id=1, source_target_pairs={{0,16},{24,8},{16,32},{40,24},{32,48},{56,40},{48,49},{57,56},{49,... | collective-permute-start | bytes 589832 | tf_op jit(solution)/shard_map/ppermute | solution.py:282
  41.9 6.5 %collective-permute-done.1.side = bf16[16,3,16,128]{3,2,1,0:T(8,128)(2,1)S(1)} collective-permute-done((bf16[16,3,16,128]{3,2,1,0:T(8,128)(2,1)S(1)}, bf16[16,3,16,128]{3,2,1,0:T(8,128)(2,1)S(1)}, u32[]{:S(2)}, u32[]{:S(2)}) %collective-permute-start.1) | collective-permute-done | bytes 196640 | tf_op jit(solution)/shard_map/ppermute | solution.py:282
  48.5 1.3 %copy.34 = bf16[256,1024]{0,1:T(8,128)(2,1)S(1)} copy(bf16[256,1024]{1,0:T(8,128)(2,1)} %param.21) | data formatting | bytes 1048576 | tf_op args[8]
  50.3 6.2 %step0.1 = (f32[16,2,16,128]{3,2,1,0:T(8,128)S(1)}, bf16[16,2,16,128]{3,2,1,0:T(8,128)(2,1)S(1)}) custom-call(s32[5,128]{1,0:T(8,128)S(1)} %copy-done.4, s32[3]{0:T(128)S(1)} %copy-done.5, bf16[16,2,16,128]{3,2,1,0:T(8,128)(2,1)S(1)} %copy-done.3, bf16[16,2,16,128]{3,2,1,0:T(8,128)(2,1)S(1)} %copy-done.3, ...), custom_call_target="tpu_custom_call" | custom-call | flops 4294967296 | bytes 4194304 | tf_op jit(solution)/shard_map/step0/pallas_call | solution.py:179
  58.1 1.9 %collective-permute-start.4 = (bf16[16,3,16,128]{3,2,1,0:T(8,128)(2,1)S(1)}, bf16[16,3,16,128]{3,2,1,0:T(8,128)(2,1)S(1)}, u32[]{:S(2)}, u32[]{:S(2)}) collective-permute-start(bf16[16,3,16,128]{3,2,1,0:T(8,128)(2,1)S(1)} %pad_maximum_fusion.2), channel_id=1, source_target_pairs={{0,16},{24,8},{16,32},{40,24},{32,48},{56,40},{48,49},{57,56},{49,... | collective-permute-start | bytes 589832 | tf_op jit(solution)/shard_map/ppermute | solution.py:282
  60.1 6.5 %collective-permute-done.4.side = bf16[16,3,16,128]{3,2,1,0:T(8,128)(2,1)S(1)} collective-permute-done((bf16[16,3,16,128]{3,2,1,0:T(8,128)(2,1)S(1)}, bf16[16,3,16,128]{3,2,1,0:T(8,128)(2,1)S(1)}, u32[]{:S(2)}, u32[]{:S(2)}) %collective-permute-start.4) | collective-permute-done | bytes 196640 | tf_op jit(solution)/shard_map/ppermute | solution.py:282
  66.6 1.2 collective-permute-done.5.other
  67.9 9.1 %step1.1 = (f32[16,2,16,128]{3,2,1,0:T(8,128)S(1)}, bf16[16,2,16,128]{3,2,1,0:T(8,128)(2,1)S(1)}) custom-call(s32[5,128]{1,0:T(8,128)S(1)} %copy-done.4, s32[3]{0:T(128)S(1)} %copy-done.5, f32[16,2,16,128]{3,2,1,0:T(8,128)S(1)} %get-tuple-element.12.own_f, bf16[16,2,16,128]{3,2,1,0:T(8,128)(2,1)S(1)} %get-tuple-element.13.own_b, ...), custom_call_target="tpu_custom_call" | custom-call | flops 4294967296 | bytes 4194304 | tf_op jit(solution)/shard_map/step1/pallas_call | solution.py:179
  77.1 1.2 collective-permute-done.6.part
  78.4 1.9 %collective-permute-start.7 = (bf16[16,3,16,128]{3,2,1,0:T(8,128)(2,1)S(1)}, bf16[16,3,16,128]{3,2,1,0:T(8,128)(2,1)S(1)}, u32[]{:S(2)}, u32[]{:S(2)}) collective-permute-start(bf16[16,3,16,128]{3,2,1,0:T(8,128)(2,1)S(1)} %pad_maximum_fusion.3), channel_id=1, source_target_pairs={{0,16},{24,8},{16,32},{40,24},{32,48},{56,40},{48,49},{57,56},{49,... | collective-permute-start | bytes 589832 | tf_op jit(solution)/shard_map/ppermute | solution.py:282
  80.3 6.5 %collective-permute-done.7.side = bf16[16,3,16,128]{3,2,1,0:T(8,128)(2,1)S(1)} collective-permute-done((bf16[16,3,16,128]{3,2,1,0:T(8,128)(2,1)S(1)}, bf16[16,3,16,128]{3,2,1,0:T(8,128)(2,1)S(1)}, u32[]{:S(2)}, u32[]{:S(2)}) %collective-permute-start.7) | collective-permute-done | bytes 196640 | tf_op jit(solution)/shard_map/ppermute | solution.py:282
  86.8 1.2 collective-permute-done.8.other
  88.1 10.0 %step2.1 = (f32[16,2,16,128]{3,2,1,0:T(8,128)S(1)}, bf16[16,2,16,128]{3,2,1,0:T(8,128)(2,1)S(1)}) custom-call(s32[5,128]{1,0:T(8,128)S(1)} %copy-done.4, s32[3]{0:T(128)S(1)} %copy-done.5, f32[16,2,16,128]{3,2,1,0:T(8,128)S(1)} %get-tuple-element.14.own_f, bf16[16,2,16,128]{3,2,1,0:T(8,128)(2,1)S(1)} %get-tuple-element.15.own_b, ...), custom_call_target="tpu_custom_call" | custom-call | flops 4294967296 | bytes 4194304 | tf_op jit(solution)/shard_map/step2/pallas_call | solution.py:179
  99.5 1.9 %collective-permute-start.10 = (bf16[16,3,16,128]{3,2,1,0:T(8,128)(2,1)S(1)}, bf16[16,3,16,128]{3,2,1,0:T(8,128)(2,1)S(1)}, u32[]{:S(2)}, u32[]{:S(2)}) collective-permute-start(bf16[16,3,16,128]{3,2,1,0:T(8,128)(2,1)S(1)} %pad_maximum_fusion.4), channel_id=1, source_target_pairs={{0,16},{24,8},{16,32},{40,24},{32,48},{56,40},{48,49},{57,56},{49,... | collective-permute-start | bytes 589832 | tf_op jit(solution)/shard_map/ppermute | solution.py:282
  101.5 6.5 %collective-permute-done.10.side = bf16[16,3,16,128]{3,2,1,0:T(8,128)(2,1)S(1)} collective-permute-done((bf16[16,3,16,128]{3,2,1,0:T(8,128)(2,1)S(1)}, bf16[16,3,16,128]{3,2,1,0:T(8,128)(2,1)S(1)}, u32[]{:S(2)}, u32[]{:S(2)}) %collective-permute-start.10) | collective-permute-done | bytes 196640 | tf_op jit(solution)/shard_map/ppermute | solution.py:282
  108.0 1.2 collective-permute-done.11.other
  109.3 12.8 %step3.1 = (f32[16,2,16,128]{3,2,1,0:T(8,128)}, bf16[16,2,16,128]{3,2,1,0:T(8,128)(2,1)}, bf16[16,2,16,128]{3,2,1,0:T(8,128)(2,1)S(1)}) custom-call(s32[5,128]{1,0:T(8,128)S(1)} %copy-done.4, s32[3]{0:T(128)S(1)} %copy-done.5, f32[16,2,16,128]{3,2,1,0:T(8,128)S(1)} %get-tuple-element.16.own_f, bf16[16,2,16,128]{3,2,1,0:T(8,128)(2,1)S(1)} %get-tuple-element.17.own_b, ...), custom_call_target="tpu_custom_call" | custom-call | flops 4294967296 | bytes 4194304 | tf_op jit(solution)/shard_map/step3/pallas_call | solution.py:179
  122.0 8.5 %all_to_all.10 = bf16[8,64,128]{2,1,0:T(8,128)(2,1)S(1)} all-to-all(bf16[8,64,128]{2,1,0:T(8,128)(2,1)S(1)} %bitcast.55), channel_id=1, replica_groups={{0,8,16,24,32,40,48,56},{64,72,80,88,96,104,112,120},{49,57,33,41,17,25..., dimensions={0} | all-to-all | bytes 262144 | tf_op jit(solution)/shard_map/all_to_all | solution.py:287
  (96 shorter events, 19.1 us)
Async XLA Ops:
  0.0 29.1 %copy-start = (bf16[1024,256]{1,0:T(8,128)(2,1)S(1)}, bf16[1024,256]{1,0:T(8,128)(2,1)}, u32[]{:S(2)}) copy-start(bf16[1024,256]{1,0:T(8,128)(2,1)} %param.23) | copy-start | bytes 1572868
  6.0 8.2 %copy-start.15 = (f32[256]{0:T(256)S(1)}, f32[256]{0:T(256)}, u32[]{:S(2)}) copy-start(f32[256]{0:T(256)} %param.18) | copy-start | bytes 3076
  6.0 9.5 %copy-start.10 = (bf16[16,256]{1,0:T(8,128)(2,1)S(1)}, bf16[16,256]{1,0:T(8,128)(2,1)}, u32[]{:S(2)}) copy-start(bf16[16,256]{1,0:T(8,128)(2,1)} %param.16) | copy-start | bytes 24580
  6.0 9.5 %copy-start.11 = (bf16[7,7,256]{2,1,0:T(8,128)(2,1)S(1)}, bf16[7,7,256]{2,1,0:T(8,128)(2,1)}, u32[]{:S(2)}) copy-start(bf16[7,7,256]{2,1,0:T(8,128)(2,1)} %param.17) | copy-start | bytes 75268
  6.1 9.8 %copy-start.8 = (bf16[256,16]{0,1:T(8,128)(2,1)S(1)}, bf16[256,16]{0,1:T(8,128)(2,1)}, u32[]{:S(2)}) copy-start(bf16[256,16]{0,1:T(8,128)(2,1)} %param.25) | copy-start | bytes 24580
  6.1 9.8 %copy-start.19 = (f32[256]{0:T(256)S(1)}, f32[256]{0:T(256)}, u32[]{:S(2)}) copy-start(f32[256]{0:T(256)} %param.24) | copy-start | bytes 3076
  6.1 29.0 %all-to-all-start = ((bf16[16,320,128]{2,1,0:T(8,128)(2,1)}), bf16[16,320,128]{2,1,0:T(8,128)(2,1)S(1)}, u32[]{:S(2)}, u32[]{:S(2)}) async-start(bf16[16,320,128]{2,1,0:T(8,128)(2,1)} %bitcast.6), calls=%async_computation | async-start | bytes 2621440 | tf_op jit(solution)/shard_map/all_to_all | solution.py:275
  29.0 9.4 %copy-start.12 = (bf16[1,16]{0,1:T(8,128)(2,1)S(1)}, bf16[1,16]{0,1:T(8,128)(2,1)}, u32[]{:S(2)}) copy-start(bf16[1,16]{0,1:T(8,128)(2,1)} %copy.35) | copy-start | bytes 100
  29.0 9.4 %copy-start.13 = (bf16[1,16]{0,1:T(8,128)(2,1)S(1)}, bf16[1,16]{0,1:T(8,128)(2,1)}, u32[]{:S(2)}) copy-start(bf16[1,16]{0,1:T(8,128)(2,1)} %copy.36) | copy-start | bytes 100
  29.0 9.4 %copy-start.18 = (bf16[32]{0:T(256)(128)(2,1)S(1)}, bf16[32]{0:T(256)(128)(2,1)}, u32[]{:S(2)}) copy-start(bf16[32]{0:T(256)(128)(2,1)} %pad.9.clone) | copy-start | bytes 196
  29.2 12.8 %copy-start.16 = (f32[256]{0:T(256)S(1)}, f32[256]{0:T(256)}, u32[]{:S(2)}) copy-start(f32[256]{0:T(256)} %param.19) | copy-start | bytes 3076
  29.2 19.3 %copy-start.17 = (f32[256]{0:T(256)S(1)}, f32[256]{0:T(256)}, u32[]{:S(2)}) copy-start(f32[256]{0:T(256)} %param.20) | copy-start | bytes 3076
  38.4 1.6 %collective-permute-start = (bf16[16,2,16,128]{3,2,1,0:T(8,128)(2,1)}, bf16[16,2,16,128]{3,2,1,0:T(8,128)(2,1)S(1)}, u32[]{:S(2)}, u32[]{:S(2)}) collective-permute-start(bf16[16,2,16,128]{3,2,1,0:T(8,128)(2,1)} %pack.1.own_f.own_b), channel_id=1, source_target_pairs={{0,8},{8,0},{16,24},{24,16},{32,40},{40,32},{48,56},{56,48},{64,72... | collective-permute-start | bytes 393224 | tf_op jit(solution)/shard_map/ppermute | solution.py:280
  40.0 8.5 %collective-permute-start.1 = (bf16[16,3,16,128]{3,2,1,0:T(8,128)(2,1)S(1)}, bf16[16,3,16,128]{3,2,1,0:T(8,128)(2,1)S(1)}, u32[]{:S(2)}, u32[]{:S(2)}) collective-permute-start(bf16[16,3,16,128]{3,2,1,0:T(8,128)(2,1)S(1)} %pad_maximum_fusion.1), channel_id=1, source_target_pairs={{0,16},{24,8},{16,32},{40,24},{32,48},{56,40},{48,49},{57,56},{49,... | collective-permute-start | bytes 589832 | tf_op jit(solution)/shard_map/ppermute | solution.py:282
  48.5 1.4 %collective-permute-start.2 = (bf16[16,16,128]{2,1,0:T(8,128)(2,1)S(1)}, bf16[16,16,128]{2,1,0:T(8,128)(2,1)S(1)}, u32[]{:S(2)}, u32[]{:S(2)}) collective-permute-start(bf16[16,16,128]{2,1,0:T(8,128)(2,1)S(1)} %dynamic-slice_bitcast_fusion.3), channel_id=1, source_target_pairs={{0,8},{8,0},{16,24},{24,16},{32,40},{40,32},{48,56},{56,48},{64,72... | collective-permute-start | bytes 196616 | tf_op jit(solution)/shard_map/ppermute | solution.py:283
  56.6 1.5 %collective-permute-start.3 = (bf16[16,2,16,128]{3,2,1,0:T(8,128)(2,1)S(1)}, bf16[16,2,16,128]{3,2,1,0:T(8,128)(2,1)S(1)}, u32[]{:S(2)}, u32[]{:S(2)}) collective-permute-start(bf16[16,2,16,128]{3,2,1,0:T(8,128)(2,1)S(1)} %get-tuple-element.13.own_b), channel_id=1, source_target_pairs={{0,8},{8,0},{16,24},{24,16},{32,40},{40,32},{48,56},{56,48},{64,72... | collective-permute-start | bytes 393224 | tf_op jit(solution)/shard_map/ppermute | solution.py:280
  58.1 8.5 %collective-permute-start.4 = (bf16[16,3,16,128]{3,2,1,0:T(8,128)(2,1)S(1)}, bf16[16,3,16,128]{3,2,1,0:T(8,128)(2,1)S(1)}, u32[]{:S(2)}, u32[]{:S(2)}) collective-permute-start(bf16[16,3,16,128]{3,2,1,0:T(8,128)(2,1)S(1)} %pad_maximum_fusion.2), channel_id=1, source_target_pairs={{0,16},{24,8},{16,32},{40,24},{32,48},{56,40},{48,49},{57,56},{49,... | collective-permute-start | bytes 589832 | tf_op jit(solution)/shard_map/ppermute | solution.py:282
  66.6 1.3 collective-permute-start.5
  76.9 1.4 %collective-permute-start.6 = (bf16[16,2,16,128]{3,2,1,0:T(8,128)(2,1)S(1)}, bf16[16,2,16,128]{3,2,1,0:T(8,128)(2,1)S(1)}, u32[]{:S(2)}, u32[]{:S(2)}) collective-permute-start(bf16[16,2,16,128]{3,2,1,0:T(8,128)(2,1)S(1)} %get-tuple-element.15.own_b), channel_id=1, source_target_pairs={{0,8},{8,0},{16,24},{24,16},{32,40},{40,32},{48,56},{56,48},{64,72... | collective-permute-start | bytes 393224 | tf_op jit(solution)/shard_map/ppermute | solution.py:280
  78.4 8.5 %collective-permute-start.7 = (bf16[16,3,16,128]{3,2,1,0:T(8,128)(2,1)S(1)}, bf16[16,3,16,128]{3,2,1,0:T(8,128)(2,1)S(1)}, u32[]{:S(2)}, u32[]{:S(2)}) collective-permute-start(bf16[16,3,16,128]{3,2,1,0:T(8,128)(2,1)S(1)} %pad_maximum_fusion.3), channel_id=1, source_target_pairs={{0,16},{24,8},{16,32},{40,24},{32,48},{56,40},{48,49},{57,56},{49,... | collective-permute-start | bytes 589832 | tf_op jit(solution)/shard_map/ppermute | solution.py:282
  86.8 1.3 collective-permute-start.8
  98.1 1.4 %collective-permute-start.9 = (bf16[16,2,16,128]{3,2,1,0:T(8,128)(2,1)S(1)}, bf16[16,2,16,128]{3,2,1,0:T(8,128)(2,1)S(1)}, u32[]{:S(2)}, u32[]{:S(2)}) collective-permute-start(bf16[16,2,16,128]{3,2,1,0:T(8,128)(2,1)S(1)} %get-tuple-element.17.own_b), channel_id=1, source_target_pairs={{0,8},{8,0},{16,24},{24,16},{32,40},{40,32},{48,56},{56,48},{64,72... | collective-permute-start | bytes 393224 | tf_op jit(solution)/shard_map/ppermute | solution.py:280
  99.5 8.5 %collective-permute-start.10 = (bf16[16,3,16,128]{3,2,1,0:T(8,128)(2,1)S(1)}, bf16[16,3,16,128]{3,2,1,0:T(8,128)(2,1)S(1)}, u32[]{:S(2)}, u32[]{:S(2)}) collective-permute-start(bf16[16,3,16,128]{3,2,1,0:T(8,128)(2,1)S(1)} %pad_maximum_fusion.4), channel_id=1, source_target_pairs={{0,16},{24,8},{16,32},{40,24},{32,48},{56,40},{48,49},{57,56},{49,... | collective-permute-start | bytes 589832 | tf_op jit(solution)/shard_map/ppermute | solution.py:282
  108.0 1.3 collective-permute-start.11
  (9 other events, 38.0 us)

commit v2 on v1

--- a/solution.py
+++ b/solution.py
@@ -6,6 +6,7 @@
 from jax.experimental import pallas as pl
 from jax.experimental.pallas import tpu as pltpu
 from jax.sharding import PartitionSpec as P
+
 
 STEPS = 4
 BF = jnp.bfloat16
@@ -71,6 +72,10 @@
         scratch_shapes=[pltpu.SMEM((steps, count), jnp.int32), pltpu.SMEM((steps, count), jnp.int32)],
         name="table",
     )(ancestors, place)
+
+
+def doubled(x):
+    return jnp.concatenate([x, x], axis=1)
 
 
 def shifted(row, off):
@@ -101,6 +106,7 @@
     bin_,
     wout,
     wskip,
+    bout,
     moved_f,
     moved_b,
     *rest,
@@ -109,7 +115,7 @@
     flip = place[2]
     ready = rest[-1]
     width = own_b.shape[3]
-    chunk = 256
+    chunk = 512
 
     def convolve(t):
         src = tab[step, SRC + t]
@@ -130,33 +136,36 @@
         stacks = [jnp.concatenate(sum(taps[r : r + 7], []) + [ones], axis=0) for r in range(2)]
         conv = jnp.dot(wconv[...], jnp.concatenate(stacks, axis=1), preferred_element_type=F32)
         spread = jnp.mean(conv * conv, axis=0, keepdims=True)
-        return (conv * lax.rsqrt(spread + 1e-06) * gain[...] + shift[...]).astype(BF)
+        return (conv * lax.rsqrt(spread + 1e-06) * doubled(gain[...]) + doubled(shift[...])).astype(BF)
 
     def finish(t, normed):
         src = tab[step, SRC + t]
-        ones = jnp.ones((16, 2 * width), BF)
         center = jnp.concatenate([own_b[src, 0], own_b[src, 1]], axis=1)
-        acc = jnp.dot(wskip[...], jnp.concatenate([center, ones], axis=0), preferred_element_type=F32)
+        acc = jnp.dot(wskip[...], center, preferred_element_type=F32) + doubled(bout[...])
         for h in range(0, win.shape[0], chunk):
             y = jnp.dot(win[h : h + chunk], normed, preferred_element_type=F32)
-            y = (y + bin_[h : h + chunk]).astype(BF)
+            y = (y + doubled(bin_[h : h + chunk])).astype(BF)
             gate = jnp.tanh(y * (y * y + BF(LINEAR))) + BF(1.0)
             acc = acc + jnp.dot(wout[:, h : h + chunk], y * gate, preferred_element_type=F32)
         q = tab[step, PARTICLE + t]
         source = (q // 2) ^ flip
+        values = []
         for r in range(2):
             value = (
                 (0.9 - 0.05 * step) * own_f[src, r].astype(F32)
                 + acc[:, r * width : (r + 1) * width]
-                + 0.3 * noise[source, 1 + step, q % 2, r].astype(F32)
+                + 0.3 * noise[source, step - 1 if step else 1, q % 2, r].astype(F32)
             )
             moved_f[t, r] = value
             moved_b[t, r] = value.astype(BF)
+            values.append(value)
+        if not last:
+            rest[0][t, 0] = lax.select(low, values[1], values[0]).astype(BF)
 
     def body(t, carry):
         normed = ready[...]
+        finish(jnp.maximum(t - 1, 0), normed)
         following = convolve(t)
-        finish(jnp.maximum(t - 1, 0), normed)
         ready[...] = following
         return carry
 
@@ -174,24 +183,25 @@
 def run_step(step, last, *operands):
     own_b, wconv = operands[3], operands[8]
     outs = [jax.ShapeDtypeStruct(own_b.shape, F32), jax.ShapeDtypeStruct(own_b.shape, BF)]
-    if last:
-        outs.append(jax.ShapeDtypeStruct(own_b.shape, BF))
+    slots, each, channels, width = own_b.shape
+    outs.append(jax.ShapeDtypeStruct((slots, each if last else 1, channels, width), BF))
     return pl.pallas_call(
         functools.partial(step_kernel, step, last),
         out_shape=outs,
         in_specs=[SMEM, SMEM] + [VMEM] * (len(operands) - 2),
         out_specs=[VMEM] * len(outs),
         scratch_shapes=[pltpu.VMEM((wconv.shape[0], 2 * own_b.shape[3]), BF)],
-        compiler_params=pltpu.CompilerParams(vmem_limit_bytes=40 << 20),
+        compiler_params=pltpu.CompilerParams(vmem_limit_bytes=16 << 20),
         cost_estimate=pl.CostEstimate(flops=4 << 30, bytes_accessed=4 << 20, transcendentals=0),
-        name=f"step{step}",
     )(*operands)
 
 
-def pack_kernel(tab, place, states, packed):
+def pack_kernel(tab, place, states, packed, near):
     def copy(i, carry):
         q = tab[0, PARTICLE + i]
-        packed[i] = states[(q // 2) ^ place[2], 0, q % 2]
+        source = (q // 2) ^ place[2]
+        packed[i] = states[source, 0, q % 2]
+        near[i, 0] = states[source, 0, q % 2, 1 - place[0]]
         return carry
 
     lax.fori_loop(0, packed.shape[0], copy, 0)
@@ -200,42 +210,128 @@
 def pack(slots, tab, place, states):
     return pl.pallas_call(
         pack_kernel,
-        out_shape=jax.ShapeDtypeStruct((slots,) + states.shape[3:], BF),
+        out_shape=[jax.ShapeDtypeStruct((slots, n) + states.shape[4:], BF) for n in (states.shape[3], 1)],
         in_specs=[SMEM, SMEM, VMEM],
-        out_specs=VMEM,
+        out_specs=[VMEM] * 2,
         name="pack",
     )(tab, place, states)
 
 
-def high_low(x):
-    high = x.astype(BF)
-    return high, (x - high.astype(F32)).astype(BF)
-
-
-def weights(embed, depth, depth_bias, gain, shift, inner, inner_bias, outer, outer_bias, head, pos):
-    hp = lax.Precision.HIGHEST
-    full = depth.astype(F32)[:, :, None, :] * embed.astype(F32)[None, None]
-    dim = full.shape[-1]
-    full = full.reshape(-1, dim)
-    full = full - jnp.mean(full, axis=-1, keepdims=True)
-    bias = depth_bias - jnp.mean(depth_bias)
-    bh, bl = high_low(bias)
-    wconv = jnp.concatenate([full.astype(BF), bh[None], bl[None], jnp.zeros((14, dim), BF)], axis=0).T
-    wide = lambda v, s: jnp.broadcast_to((v * s)[:, None], (v.shape[0], pos))
-    head_f = head.astype(F32)
-    wout = (jnp.dot(outer.astype(F32), head_f, precision=hp) * (0.3 * SCALE)).astype(BF).T
-    wskip = 0.6 * jnp.dot(embed.astype(F32), head_f, precision=hp)
-    oh, ol = high_low(0.6 * jnp.dot(outer_bias[None], head_f, precision=hp))
-    wskip = jnp.concatenate([wskip.astype(BF), oh, ol, jnp.zeros((14, head.shape[1]), BF)], axis=0).T
-    return (
-        wconv,
-        wide(gain, 1.0 / SCALE),
-        wide(shift, 1.0 / SCALE),
-        inner.T,
-        wide(inner_bias, 1.0 / SCALE),
-        wout,
-        wskip,
+def column(row, lanes):
+    return jnp.broadcast_to(row, (lanes, row.shape[1])).T
+
+
+def across(a, b):
+    return lax.dot_general(a, b, (((1,), (1,)), ((), ())), preferred_element_type=F32)
+
+
+def weights_kernel(
+    embed,
+    depth,
+    depth_bias,
+    gain,
+    shift,
+    inner,
+    inner_bias,
+    outer,
+    outer_bias,
+    head_t,
+    wconv,
+    gain_c,
+    shift_c,
+    win,
+    bin_c,
+    wout,
+    wskip,
+    bout,
+):
+    dim = embed.shape[1]
+    lanes = gain_c.shape[1]
+    source = embed[...].astype(F32)
+    diag = lax.broadcasted_iota(jnp.int32, (dim, dim), 0) == lax.broadcasted_iota(jnp.int32, (dim, dim), 1)
+    eye = diag.astype(F32).astype(BF)
+    taps = []
+    for i in range(depth.shape[0]):
+        line = depth[i].astype(F32)
+        for j in range(depth.shape[1]):
+            full = source * line[j : j + 1]
+            taps.append((full - jnp.mean(full, axis=1, keepdims=True)).astype(BF))
+    bias = depth_bias[...] - jnp.mean(depth_bias[...], axis=1, keepdims=True)
+    high = bias.astype(BF).astype(F32)
+    index = lax.broadcasted_iota(jnp.int32, (16, dim), 0)
+    extra = jnp.where(index == 0, high, jnp.where(index == 1, bias - high, 0.0))
+    wconv[...] = across(eye, jnp.concatenate(taps + [extra.astype(BF)], axis=0)).astype(BF)
+    gain_c[...] = column(gain[...] * (1.0 / SCALE), lanes)
+    shift_c[...] = column(shift[...] * (1.0 / SCALE), lanes)
+    for h in range(0, inner.shape[1], dim):
+        win[h : h + dim] = across(eye, inner[:, h : h + dim]).astype(BF)
+        bin_c[h : h + dim] = column(inner_bias[:, h : h + dim] * (1.0 / SCALE), lanes)
+        wout[:, h : h + dim] = (across(head_t[...], outer[h : h + dim]) * (0.3 * SCALE)).astype(BF)
+    wskip[...] = (across(head_t[...], embed[...]) * 0.6).astype(BF)
+    offset = 0.6 * jnp.sum(head_t[...].astype(F32) * outer_bias[...], axis=1, keepdims=True)
+    bout[...] = jnp.broadcast_to(offset, bout.shape)
+
+
+def weights(embed, depth, depth_bias, gain, shift, inner, inner_bias, outer, outer_bias, head, lanes):
+    channels, dim = embed.shape
+    hidden = inner.shape[1]
+    taps = depth.shape[0] * depth.shape[1] * channels + 16
+    shapes = [
+        ((dim, taps), BF),
+        ((dim, lanes), F32),
+        ((dim, lanes), F32),
+        ((hidden, dim), BF),
+        ((hidden, lanes), F32),
+        ((channels, hidden), BF),
+        ((channels, channels), BF),
+        ((channels, lanes), F32),
+    ]
+    return pl.pallas_call(
+        weights_kernel,
+        out_shape=[jax.ShapeDtypeStruct(*shape) for shape in shapes],
+        in_specs=[VMEM] * 10,
+        out_specs=[VMEM] * len(shapes),
+        compiler_params=pltpu.CompilerParams(vmem_limit_bytes=16 << 20),
+        name="weights",
+    )(
+        embed,
+        depth,
+        depth_bias[None],
+        gain[None],
+        shift[None],
+        inner,
+        inner_bias[None],
+        outer,
+        outer_bias[None],
+        head.T,
     )
+
+
+def spread_kernel(each, *refs):
+    ins, out = refs[:-1], refs[-1]
+    half = out.shape[0] // 2
+    rows = half * each
+    channels = out.shape[4]
+    images = [ref.at[a] for ref in ins for a in range(ref.shape[0])]
+    here = out.shape[2]
+    for n, image in enumerate(images):
+        for r in range(rows):
+            tile = image[pl.ds(r, channels, stride=rows), :].astype(BF)
+            for h in range(2):
+                out[h * half + r // each, n // here, n % here, r % each] = tile
+
+
+def spread_rows(parts, here, each, *arrays):
+    channels, rows, width = arrays[0].shape[1:]
+    images = sum(x.shape[0] for x in arrays)
+    return pl.pallas_call(
+        functools.partial(spread_kernel, each),
+        out_shape=jax.ShapeDtypeStruct((parts, images // here, here, each, channels, width), BF),
+        in_specs=[VMEM] * len(arrays),
+        out_specs=VMEM,
+        compiler_params=pltpu.CompilerParams(vmem_limit_bytes=16 << 20),
+        name="spread",
+    )(*[x.reshape(x.shape[0], channels * rows, width) for x in arrays])
 
 
 def per_device(latent, ancestors, noise, embed, depth, depth_bias, gain, shift, inner, inner_bias, outer, outer_bias, head):
@@ -268,22 +364,30 @@
     core = at % 2
     place = jnp.stack([core, at // half, (lax.axis_index("slab") % 2) * (half - 2)]).astype(jnp.int32)
     tab = make_table(ancestors, place, half * here)
-    stacked = jnp.concatenate([latent[None].astype(BF), noise.astype(BF)], axis=0)
     each = rows // half
-    stacked = stacked.reshape(STEPS + 1, here, channels, half, each, width).transpose(3, 0, 1, 4, 2, 5)
-    outgoing = jnp.concatenate([stacked, stacked], axis=0).reshape(parts, -1, width)
-    incoming = lax.all_to_all(outgoing, both, split_axis=0, concat_axis=0, axis_index_groups=columns, tiled=True)
-    incoming = incoming.reshape(parts, STEPS + 1, here, each, channels, width)
-    params = weights(embed, depth, depth_bias, gain, shift, inner, inner_bias, outer, outer_bias, head, each * width)
-    own_f = own_b = pack(half * here, tab, place, incoming)
+
+    def deliver(x):
+        x = x.reshape(parts, -1, width)
+        x = lax.all_to_all(x, both, split_axis=0, concat_axis=0, axis_index_groups=columns, tiled=True)
+        return x.reshape(parts, -1, here, each, channels, width)
+
+    flat = noise.reshape((-1,) + noise.shape[2:])
+    params = weights(embed, depth, depth_bias, gain, shift, inner, inner_bias, outer, outer_bias, head, width)
+    first = spread_rows(parts, here, each, latent, flat[:here])
+    later = spread_rows(parts, here, each, flat[here:])
+    first = deliver(first)
+    later = deliver(later)
+    first, params = lax.optimization_barrier((first, params))
+    own_b, near = pack(half * here, tab, place, first)
+    own_f = own_b
     for step in range(STEPS):
         part = lax.ppermute(own_b, "particle", swapped)
-        near = lax.dynamic_slice_in_dim(own_b, 1 - core, 1, axis=1)
         side = lax.ppermute(jnp.concatenate([near, part], axis=1), both, sides)
         other = lax.ppermute(lax.dynamic_index_in_dim(side, 2 - core, axis=1, keepdims=False), "particle", swapped)
-        outs = run_step(step, step == STEPS - 1, tab, place, own_f, own_b, part, side, other, incoming, *params)
-        own_f, own_b = outs[0], outs[1]
-    final = outs[2].reshape(half, -1, width)
+        drawn = first if step == 0 else later
+        outs = run_step(step, step == STEPS - 1, tab, place, own_f, own_b, part, side, other, drawn, *params)
+        own_f, own_b, near = outs
+    final = near.reshape(half, -1, width)
     home = lax.all_to_all(final, both, split_axis=0, concat_axis=0, axis_index_groups=halves, tiled=True)
     home = home.reshape(half, here, each, channels, width).transpose(1, 3, 0, 2, 4)
     return home.reshape(here, channels, rows, width).astype(F32)
@@ -296,4 +400,5 @@
         P(None, "particle", None, "slab", None),
     ) + (P(),) * 10
     out_specs = P("particle", None, "slab", None)
+
     return jax.shard_map(per_device, mesh=mesh, in_specs=in_specs, out_specs=out_specs, check_vma=False)

time: 134 us -> 119 us (0.89)
  the two profiles are of different devices: /device:TPU:2 before, /device:TPU:22 now
where the time goes in v2:
time: 119 us; the launch traced here: 118 us
  Pallas kernels  39.4 us (33%)
  waiting for transfers between devices  34.5 us (29%)
  starting transfers between devices  25.5 us (21%)
  blocking collectives  8.48 us (7%)
  local copies, waits for them, and re-layouts  8.12 us (7%)
  other arithmetic  1.58 us (1%)
    pallas_call x4, Pallas kernels, run_step(): pl.pallas_call(functools.partial(step_kernel, step, last), out_shape=outs...  29.7 us
    ppermute x4, waiting for transfers between devices, per_device(): side = lax.ppermute(jnp.concatenate([near, part], axis=1), both, sides)  24 us
    all_to_all x2, starting transfers between devices, deliver(): lax.all_to_all(x, both, split_axis=0, concat_axis=0, axis_index_groups=co...  15 us
    ppermute x4, starting transfers between devices, per_device(): side = lax.ppermute(jnp.concatenate([near, part], axis=1), both, sides)  9.78 us
    all_to_all x1, blocking collectives, per_device(): lax.all_to_all(final, both, split_axis=0, concat_axis=0, axis_index_group...  8.48 us
    ppermute x4, waiting for transfers between devices, per_device(): part = lax.ppermute(own_b, 'particle', swapped)  5.08 us
    pallas_call x1, Pallas kernels, make_table(): pl.pallas_call(functools.partial(table_kernel, final_count), out_shape=ja...  5.06 us
    unnamed x52, local copies, waits for them, and re-layouts  4.46 us
  transfers between devices with their start and end apart: 14, of which 12 were waited for; matrix products, arithmetic and copies ran while one was open for 2% of the time, Pallas kernels for 10%

profile of v2, /device:TPU:22, one launch (start us, length us, event | category | flops | bytes accessed | tf_op | source)
XLA Modules:
  0.0 118.0 jit_solution(7494141949867105672)
XLA Ops:
  2.0 8.4 %all-to-all-start = ((bf16[16,128,128]{2,1,0:T(8,128)(2,1)}), bf16[16,128,128]{2,1,0:T(8,128)(2,1)S(1)}, u32[]{:S(2)}, u32[]{:S(2)}) async-start(bf16[16,128,128]{2,1,0:T(8,128)(2,1)} %bitcast.5), calls=%async_computation | async-start | bytes 1048576 | tf_op jit(solution)/shard_map/all_to_all | solution.py:371
  11.1 5.1 %table.1.tab = s32[5,128]{1,0:T(8,128)} custom-call(s32[4,32]{1,0:T(4,128)} %anc.1, s32[3]{0:T(128)} %pad_add_fusion.place), custom_call_target="tpu_custom_call" | custom-call | tf_op jit(solution)/shard_map/table/pallas_call | solution.py:67
  18.2 1.7 %all-to-all-done = bf16[16,128,128]{2,1,0:T(8,128)(2,1)S(1)} async-done(((bf16[16,128,128]{2,1,0:T(8,128)(2,1)}), bf16[16,128,128]{2,1,0:T(8,128)(2,1)S(1)}, u32[]{:S(2)}, u32[]{:S(2)}) %all-to-all-start) | async-done | bytes 524320 | tf_op jit(solution)/shard_map/all_to_all | solution.py:371
  20.7 1.9 %pack.1 = (bf16[16,2,16,128]{3,2,1,0:T(8,128)(2,1)}, bf16[16,1,16,128]{3,2,1,0:T(8,128)(2,1)}) custom-call(s32[5,128]{1,0:T(8,128)} %table.1.tab, s32[3]{0:T(128)} %pad_add_fusion.place, bf16[16,2,2,2,16,128]{5,4,3,2,1,0:T(8,128)(2,1)} %bitcast.31), custom_call_target="tpu_custom_call" | custom-call | tf_op jit(solution)/shard_map/pack/pallas_call | solution.py:211
  22.7 1.4 %collective-permute-done.part = bf16[16,2,16,128]{3,2,1,0:T(8,128)(2,1)S(1)} collective-permute-done((bf16[16,2,16,128]{3,2,1,0:T(8,128)(2,1)}, bf16[16,2,16,128]{3,2,1,0:T(8,128)(2,1)S(1)}, u32[]{:S(2)}, u32[]{:S(2)}) %collective-permute-start) | collective-permute-done | bytes 131104 | tf_op jit(solution)/shard_map/ppermute | solution.py:384
  25.0 2.0 %collective-permute-start.1 = (bf16[16,3,16,128]{3,2,1,0:T(8,128)(2,1)S(1)}, bf16[16,3,16,128]{3,2,1,0:T(8,128)(2,1)S(1)}, u32[]{:S(2)}, u32[]{:S(2)}) collective-permute-start(bf16[16,3,16,128]{3,2,1,0:T(8,128)(2,1)S(1)} %pad_maximum_fusion), channel_id=1, source_target_pairs={{0,16},{24,8},{16,32},{40,24},{32,48},{56,40},{48,49},{57,56},{49,... | collective-permute-start | bytes 589832 | tf_op jit(solution)/shard_map/ppermute | solution.py:385
  27.1 6.4 %collective-permute-done.1.side = bf16[16,3,16,128]{3,2,1,0:T(8,128)(2,1)S(1)} collective-permute-done((bf16[16,3,16,128]{3,2,1,0:T(8,128)(2,1)S(1)}, bf16[16,3,16,128]{3,2,1,0:T(8,128)(2,1)S(1)}, u32[]{:S(2)}, u32[]{:S(2)}) %collective-permute-start.1) | collective-permute-done | bytes 196640 | tf_op jit(solution)/shard_map/ppermute | solution.py:385
  36.5 6.6 %all-to-all-start.1 = ((bf16[16,192,128]{2,1,0:T(8,128)(2,1)}), bf16[16,192,128]{2,1,0:T(8,128)(2,1)S(1)}, u32[]{:S(2)}, u32[]{:S(2)}) async-start(bf16[16,192,128]{2,1,0:T(8,128)(2,1)} %bitcast.16), calls=%async_computation.1 | async-start | bytes 1572864 | tf_op jit(solution)/shard_map/all_to_all | solution.py:371
  44.5 5.2 %shard_map.127 = (f32[16,2,16,128]{3,2,1,0:T(8,128)S(1)}, bf16[16,2,16,128]{3,2,1,0:T(8,128)(2,1)S(1)}, bf16[16,1,16,128]{3,2,1,0:T(8,128)(2,1)S(1)}) custom-call(s32[5,128]{1,0:T(8,128)S(1)} %copy-done.6, s32[3]{0:T(128)S(1)} %copy-done.9, bf16[16,2,16,128]{3,2,1,0:T(8,128)(2,1)S(1)} %copy-done.15, bf16[16,2,16,128]{3,2,1,0:T(8,128)(2,1)S(1)} %copy-done.15, ...), custom_call_target="tpu_custom_call" | custom-call | flops 4294967296 | bytes 4194304 | tf_op jit(solution)/shard_map/pallas_call | solution.py:188
  50.0 1.2 %collective-permute-done.3.part = bf16[16,2,16,128]{3,2,1,0:T(8,128)(2,1)S(1)} collective-permute-done((bf16[16,2,16,128]{3,2,1,0:T(8,128)(2,1)S(1)}, bf16[16,2,16,128]{3,2,1,0:T(8,128)(2,1)S(1)}, u32[]{:S(2)}, u32[]{:S(2)}) %collective-permute-start.3) | collective-permute-done | bytes 131104 | tf_op jit(solution)/shard_map/ppermute | solution.py:384
  51.3 3.4 %collective-permute-start.4 = (bf16[16,3,16,128]{3,2,1,0:T(8,128)(2,1)S(1)}, bf16[16,3,16,128]{3,2,1,0:T(8,128)(2,1)S(1)}, u32[]{:S(2)}, u32[]{:S(2)}) collective-permute-start(bf16[16,3,16,128]{3,2,1,0:T(8,128)(2,1)S(1)} %pad_maximum_fusion.1), channel_id=1, source_target_pairs={{0,16},{24,8},{16,32},{40,24},{32,48},{56,40},{48,49},{57,56},{49,... | collective-permute-start | bytes 589832 | tf_op jit(solution)/shard_map/ppermute | solution.py:385
  54.7 5.1 %collective-permute-done.4.side = bf16[16,3,16,128]{3,2,1,0:T(8,128)(2,1)S(1)} collective-permute-done((bf16[16,3,16,128]{3,2,1,0:T(8,128)(2,1)S(1)}, bf16[16,3,16,128]{3,2,1,0:T(8,128)(2,1)S(1)}, u32[]{:S(2)}, u32[]{:S(2)}) %collective-permute-start.4) | collective-permute-done | bytes 196640 | tf_op jit(solution)/shard_map/ppermute | solution.py:385
  59.8 1.2 %collective-permute-done.5.other = bf16[16,16,128]{2,1,0:T(8,128)(2,1)S(1)} collective-permute-done((bf16[16,16,128]{2,1,0:T(8,128)(2,1)S(1)}, bf16[16,16,128]{2,1,0:T(8,128)(2,1)S(1)}, u32[]{:S(2)}, u32[]{:S(2)}) %collective-permute-start.5) | collective-permute-done | bytes 65568 | tf_op jit(solution)/shard_map/ppermute | solution.py:386
  62.0 5.7 %shard_map.128 = (f32[16,2,16,128]{3,2,1,0:T(8,128)S(1)}, bf16[16,2,16,128]{3,2,1,0:T(8,128)(2,1)S(1)}, bf16[16,1,16,128]{3,2,1,0:T(8,128)(2,1)S(1)}) custom-call(s32[5,128]{1,0:T(8,128)S(1)} %copy-done.6, s32[3]{0:T(128)S(1)} %copy-done.9, f32[16,2,16,128]{3,2,1,0:T(8,128)S(1)} %copy-done.25, bf16[16,2,16,128]{3,2,1,0:T(8,128)(2,1)S(1)} %copy-done.17, ...), custom_call_target="tpu_custom_call" | custom-call | flops 4294967296 | bytes 4194304 | tf_op jit(solution)/shard_map/pallas_call | solution.py:188
  67.9 1.2 %collective-permute-done.6.part = bf16[16,2,16,128]{3,2,1,0:T(8,128)(2,1)S(1)} collective-permute-done((bf16[16,2,16,128]{3,2,1,0:T(8,128)(2,1)S(1)}, bf16[16,2,16,128]{3,2,1,0:T(8,128)(2,1)S(1)}, u32[]{:S(2)}, u32[]{:S(2)}) %collective-permute-start.6) | collective-permute-done | bytes 131104 | tf_op jit(solution)/shard_map/ppermute | solution.py:384
  69.1 2.5 %collective-permute-start.7 = (bf16[16,3,16,128]{3,2,1,0:T(8,128)(2,1)S(1)}, bf16[16,3,16,128]{3,2,1,0:T(8,128)(2,1)S(1)}, u32[]{:S(2)}, u32[]{:S(2)}) collective-permute-start(bf16[16,3,16,128]{3,2,1,0:T(8,128)(2,1)S(1)} %pad_maximum_fusion.2), channel_id=1, source_target_pairs={{0,16},{24,8},{16,32},{40,24},{32,48},{56,40},{48,49},{57,56},{49,... | collective-permute-start | bytes 589832 | tf_op jit(solution)/shard_map/ppermute | solution.py:385
  71.6 6.0 %collective-permute-done.7.side = bf16[16,3,16,128]{3,2,1,0:T(8,128)(2,1)S(1)} collective-permute-done((bf16[16,3,16,128]{3,2,1,0:T(8,128)(2,1)S(1)}, bf16[16,3,16,128]{3,2,1,0:T(8,128)(2,1)S(1)}, u32[]{:S(2)}, u32[]{:S(2)}) %collective-permute-start.7) | collective-permute-done | bytes 196640 | tf_op jit(solution)/shard_map/ppermute | solution.py:385
  77.6 1.2 %collective-permute-done.8.other = bf16[16,16,128]{2,1,0:T(8,128)(2,1)S(1)} collective-permute-done((bf16[16,16,128]{2,1,0:T(8,128)(2,1)S(1)}, bf16[16,16,128]{2,1,0:T(8,128)(2,1)S(1)}, u32[]{:S(2)}, u32[]{:S(2)}) %collective-permute-start.8) | collective-permute-done | bytes 65568 | tf_op jit(solution)/shard_map/ppermute | solution.py:386
  78.9 7.8 %shard_map.129 = (f32[16,2,16,128]{3,2,1,0:T(8,128)S(1)}, bf16[16,2,16,128]{3,2,1,0:T(8,128)(2,1)S(1)}, bf16[16,1,16,128]{3,2,1,0:T(8,128)(2,1)S(1)}) custom-call(s32[5,128]{1,0:T(8,128)S(1)} %copy-done.6, s32[3]{0:T(128)S(1)} %copy-done.9, f32[16,2,16,128]{3,2,1,0:T(8,128)S(1)} %get-tuple-element.56.own_f, ...), custom_call_target="tpu_custom_call" | custom-call | flops 4294967296 | bytes 4194304 | tf_op jit(solution)/shard_map/pallas_call | solution.py:188
  88.1 1.9 %collective-permute-start.10 = (bf16[16,3,16,128]{3,2,1,0:T(8,128)(2,1)S(1)}, bf16[16,3,16,128]{3,2,1,0:T(8,128)(2,1)S(1)}, u32[]{:S(2)}, u32[]{:S(2)}) collective-permute-start(bf16[16,3,16,128]{3,2,1,0:T(8,128)(2,1)S(1)} %pad_maximum_fusion.3), channel_id=1, source_target_pairs={{0,16},{24,8},{16,32},{40,24},{32,48},{56,40},{48,49},{57,56},{49,... | collective-permute-start | bytes 589832 | tf_op jit(solution)/shard_map/ppermute | solution.py:385
  90.0 6.5 %collective-permute-done.10.side = bf16[16,3,16,128]{3,2,1,0:T(8,128)(2,1)S(1)} collective-permute-done((bf16[16,3,16,128]{3,2,1,0:T(8,128)(2,1)S(1)}, bf16[16,3,16,128]{3,2,1,0:T(8,128)(2,1)S(1)}, u32[]{:S(2)}, u32[]{:S(2)}) %collective-permute-start.10) | collective-permute-done | bytes 196640 | tf_op jit(solution)/shard_map/ppermute | solution.py:385
  96.6 1.2 %collective-permute-done.11.other = bf16[16,16,128]{2,1,0:T(8,128)(2,1)S(1)} collective-permute-done((bf16[16,16,128]{2,1,0:T(8,128)(2,1)S(1)}, bf16[16,16,128]{2,1,0:T(8,128)(2,1)S(1)}, u32[]{:S(2)}, u32[]{:S(2)}) %collective-permute-start.11) | collective-permute-done | bytes 65568 | tf_op jit(solution)/shard_map/ppermute | solution.py:386
  97.8 10.9 %shard_map.130 = (f32[16,2,16,128]{3,2,1,0:T(8,128)}, bf16[16,2,16,128]{3,2,1,0:T(8,128)(2,1)}, bf16[16,2,16,128]{3,2,1,0:T(8,128)(2,1)S(1)}) custom-call(s32[5,128]{1,0:T(8,128)S(1)} %copy-done.6, s32[3]{0:T(128)S(1)} %copy-done.9, f32[16,2,16,128]{3,2,1,0:T(8,128)S(1)} %get-tuple-element.59.own_f, bf16[16,2,16,128]{3,2,1,0:T(8,128)(2,1)S(1)} %get-tuple-element.60.own_b, ...), custom_call_target="tpu_custom_call" | custom-call | flops 4294967296 | bytes 4194304 | tf_op jit(solution)/shard_map/pallas_call | solution.py:188
  108.7 8.5 %all_to_all.15 = bf16[8,64,128]{2,1,0:T(8,128)(2,1)S(1)} all-to-all(bf16[8,64,128]{2,1,0:T(8,128)(2,1)S(1)} %bitcast.38), channel_id=1, replica_groups={{0,8,16,24,32,40,48,56},{64,72,80,88,96,104,112,120},{49,57,33,41,17,25..., dimensions={0} | all-to-all | bytes 262144 | tf_op jit(solution)/shard_map/all_to_all | solution.py:391
  (78 shorter events, 14.4 us)
Async XLA Ops:
  2.0 14.2 %copy-start.2 = (bf16[256,1024]{1,0:T(8,128)(2,1)S(1)}, bf16[256,1024]{1,0:T(8,128)(2,1)}, u32[]{:S(2)}) copy-start(bf16[256,1024]{1,0:T(8,128)(2,1)} %inner.1) | copy-start | bytes 1572868
  2.0 14.2 %copy-start.3 = (bf16[1024,256]{1,0:T(8,128)(2,1)S(1)}, bf16[1024,256]{1,0:T(8,128)(2,1)}, u32[]{:S(2)}) copy-start(bf16[1024,256]{1,0:T(8,128)(2,1)} %outer.1) | copy-start | bytes 1572868
  2.0 17.9 %all-to-all-start = ((bf16[16,128,128]{2,1,0:T(8,128)(2,1)}), bf16[16,128,128]{2,1,0:T(8,128)(2,1)S(1)}, u32[]{:S(2)}, u32[]{:S(2)}) async-start(bf16[16,128,128]{2,1,0:T(8,128)(2,1)} %bitcast.5), calls=%async_computation | async-start | bytes 1048576 | tf_op jit(solution)/shard_map/all_to_all | solution.py:371
  22.6 1.6 %collective-permute-start = (bf16[16,2,16,128]{3,2,1,0:T(8,128)(2,1)}, bf16[16,2,16,128]{3,2,1,0:T(8,128)(2,1)S(1)}, u32[]{:S(2)}, u32[]{:S(2)}) collective-permute-start(bf16[16,2,16,128]{3,2,1,0:T(8,128)(2,1)} %get-tuple-element.43.own_f.own_b), channel_id=1, source_target_pairs={{0,8},{8,0},{16,24},{24,16},{32,40},{40,32},{48,56},{56,48},{64,72... | collective-permute-start | bytes 393224 | tf_op jit(solution)/shard_map/ppermute | solution.py:384
  25.0 8.5 %collective-permute-start.1 = (bf16[16,3,16,128]{3,2,1,0:T(8,128)(2,1)S(1)}, bf16[16,3,16,128]{3,2,1,0:T(8,128)(2,1)S(1)}, u32[]{:S(2)}, u32[]{:S(2)}) collective-permute-start(bf16[16,3,16,128]{3,2,1,0:T(8,128)(2,1)S(1)} %pad_maximum_fusion), channel_id=1, source_target_pairs={{0,16},{24,8},{16,32},{40,24},{32,48},{56,40},{48,49},{57,56},{49,... | collective-permute-start | bytes 589832 | tf_op jit(solution)/shard_map/ppermute | solution.py:385
  34.1 8.9 %collective-permute-start.2 = (bf16[16,16,128]{2,1,0:T(8,128)(2,1)}, bf16[16,16,128]{2,1,0:T(8,128)(2,1)}, u32[]{:S(2)}, u32[]{:S(2)}) collective-permute-start(bf16[16,16,128]{2,1,0:T(8,128)(2,1)} %dynamic-slice_bitcast_fusion.3), channel_id=1, source_target_pairs={{0,8},{8,0},{16,24},{24,16},{32,40},{40,32},{48,56},{56,48},{64,72... | collective-permute-start | bytes 196616 | tf_op jit(solution)/shard_map/ppermute | solution.py:386
  36.5 6.6 %copy-start.1 = (bf16[16,128,128]{2,1,0:T(8,128)(2,1)S(1)}, bf16[16,128,128]{2,1,0:T(8,128)(2,1)}, u32[]{:S(2)}) copy-start(bf16[16,128,128]{2,1,0:T(8,128)(2,1)} %copy-done) | copy-start | bytes 1572868
  36.5 6.6 %copy-start.6 = (s32[5,128]{1,0:T(8,128)S(1)}, s32[5,128]{1,0:T(8,128)}, u32[]{:S(2)}) copy-start(s32[5,128]{1,0:T(8,128)} %table.1.tab) | copy-start | bytes 7684
  36.5 6.6 %copy-start.9 = (s32[3]{0:T(128)S(1)}, s32[3]{0:T(128)}, u32[]{:S(2)}) copy-start(s32[3]{0:T(128)} %pad_add_fusion.place) | copy-start | bytes 40
  36.5 6.6 %copy-start.15 = (bf16[16,2,16,128]{3,2,1,0:T(8,128)(2,1)S(1)}, bf16[16,2,16,128]{3,2,1,0:T(8,128)(2,1)}, u32[]{:S(2)}) copy-start(bf16[16,2,16,128]{3,2,1,0:T(8,128)(2,1)} %get-tuple-element.43.own_f.own_b) | copy-start | bytes 393220
  36.5 23.3 %all-to-all-start.1 = ((bf16[16,192,128]{2,1,0:T(8,128)(2,1)}), bf16[16,192,128]{2,1,0:T(8,128)(2,1)S(1)}, u32[]{:S(2)}, u32[]{:S(2)}) async-start(bf16[16,192,128]{2,1,0:T(8,128)(2,1)} %bitcast.16), calls=%async_computation.1 | async-start | bytes 1572864 | tf_op jit(solution)/shard_map/all_to_all | solution.py:371
  49.8 10.0 %copy-start.24 = (f32[16,2,16,128]{3,2,1,0:T(8,128)}, f32[16,2,16,128]{3,2,1,0:T(8,128)S(1)}, u32[]{:S(2)}) copy-start(f32[16,2,16,128]{3,2,1,0:T(8,128)S(1)} %get-tuple-element.53.own_f) | copy-start | bytes 786436
  49.8 1.4 %collective-permute-start.3 = (bf16[16,2,16,128]{3,2,1,0:T(8,128)(2,1)S(1)}, bf16[16,2,16,128]{3,2,1,0:T(8,128)(2,1)S(1)}, u32[]{:S(2)}, u32[]{:S(2)}) collective-permute-start(bf16[16,2,16,128]{3,2,1,0:T(8,128)(2,1)S(1)} %get-tuple-element.54.own_b), channel_id=1, source_target_pairs={{0,8},{8,0},{16,24},{24,16},{32,40},{40,32},{48,56},{56,48},{64,72... | collective-permute-start | bytes 393224 | tf_op jit(solution)/shard_map/ppermute | solution.py:384
  51.2 9.9 %copy-start.20 = (bf16[16,1024]{1,0:T(8,128)(2,1)S(1)}, bf16[16,1024]{1,0:T(8,128)(2,1)}, u32[]{:S(2)}) copy-start(bf16[16,1024]{1,0:T(8,128)(2,1)} %copy-done.18) | copy-start | bytes 98308
  51.3 9.8 %copy-start.23 = (bf16[16,16]{1,0:T(8,128)(2,1)S(1)}, bf16[16,16]{1,0:T(8,128)(2,1)}, u32[]{:S(2)}) copy-start(bf16[16,16]{1,0:T(8,128)(2,1)} %copy-done.21) | copy-start | bytes 1540
  51.3 8.5 %collective-permute-start.4 = (bf16[16,3,16,128]{3,2,1,0:T(8,128)(2,1)S(1)}, bf16[16,3,16,128]{3,2,1,0:T(8,128)(2,1)S(1)}, u32[]{:S(2)}, u32[]{:S(2)}) collective-permute-start(bf16[16,3,16,128]{3,2,1,0:T(8,128)(2,1)S(1)} %pad_maximum_fusion.1), channel_id=1, source_target_pairs={{0,16},{24,8},{16,32},{40,24},{32,48},{56,40},{48,49},{57,56},{49,... | collective-permute-start | bytes 589832 | tf_op jit(solution)/shard_map/ppermute | solution.py:385
  54.7 6.4 %copy-start.17 = (bf16[16,2,16,128]{3,2,1,0:T(8,128)(2,1)S(1)}, bf16[16,2,16,128]{3,2,1,0:T(8,128)(2,1)}, u32[]{:S(2)}) copy-start(bf16[16,2,16,128]{3,2,1,0:T(8,128)(2,1)} %copy-done.16) | copy-start | bytes 393220
  59.7 1.3 %collective-permute-start.5 = (bf16[16,16,128]{2,1,0:T(8,128)(2,1)S(1)}, bf16[16,16,128]{2,1,0:T(8,128)(2,1)S(1)}, u32[]{:S(2)}, u32[]{:S(2)}) collective-permute-start(bf16[16,16,128]{2,1,0:T(8,128)(2,1)S(1)} %dynamic-slice_bitcast_fusion.2), channel_id=1, source_target_pairs={{0,8},{8,0},{16,24},{24,16},{32,40},{40,32},{48,56},{56,48},{64,72... | collective-permute-start | bytes 196616 | tf_op jit(solution)/shard_map/ppermute | solution.py:386
  67.7 1.4 %collective-permute-start.6 = (bf16[16,2,16,128]{3,2,1,0:T(8,128)(2,1)S(1)}, bf16[16,2,16,128]{3,2,1,0:T(8,128)(2,1)S(1)}, u32[]{:S(2)}, u32[]{:S(2)}) collective-permute-start(bf16[16,2,16,128]{3,2,1,0:T(8,128)(2,1)S(1)} %get-tuple-element.57.own_b), channel_id=1, source_target_pairs={{0,8},{8,0},{16,24},{24,16},{32,40},{40,32},{48,56},{56,48},{64,72... | collective-permute-start | bytes 393224 | tf_op jit(solution)/shard_map/ppermute | solution.py:384
  69.1 8.5 %collective-permute-start.7 = (bf16[16,3,16,128]{3,2,1,0:T(8,128)(2,1)S(1)}, bf16[16,3,16,128]{3,2,1,0:T(8,128)(2,1)S(1)}, u32[]{:S(2)}, u32[]{:S(2)}) collective-permute-start(bf16[16,3,16,128]{3,2,1,0:T(8,128)(2,1)S(1)} %pad_maximum_fusion.2), channel_id=1, source_target_pairs={{0,16},{24,8},{16,32},{40,24},{32,48},{56,40},{48,49},{57,56},{49,... | collective-permute-start | bytes 589832 | tf_op jit(solution)/shard_map/ppermute | solution.py:385
  77.6 1.3 %collective-permute-start.8 = (bf16[16,16,128]{2,1,0:T(8,128)(2,1)S(1)}, bf16[16,16,128]{2,1,0:T(8,128)(2,1)S(1)}, u32[]{:S(2)}, u32[]{:S(2)}) collective-permute-start(bf16[16,16,128]{2,1,0:T(8,128)(2,1)S(1)} %dynamic-slice_bitcast_fusion.1), channel_id=1, source_target_pairs={{0,8},{8,0},{16,24},{24,16},{32,40},{40,32},{48,56},{56,48},{64,72... | collective-permute-start | bytes 196616 | tf_op jit(solution)/shard_map/ppermute | solution.py:386
  86.7 1.4 %collective-permute-start.9 = (bf16[16,2,16,128]{3,2,1,0:T(8,128)(2,1)S(1)}, bf16[16,2,16,128]{3,2,1,0:T(8,128)(2,1)S(1)}, u32[]{:S(2)}, u32[]{:S(2)}) collective-permute-start(bf16[16,2,16,128]{3,2,1,0:T(8,128)(2,1)S(1)} %get-tuple-element.60.own_b), channel_id=1, source_target_pairs={{0,8},{8,0},{16,24},{24,16},{32,40},{40,32},{48,56},{56,48},{64,72... | collective-permute-start | bytes 393224 | tf_op jit(solution)/shard_map/ppermute | solution.py:384
  88.1 8.5 %collective-permute-start.10 = (bf16[16,3,16,128]{3,2,1,0:T(8,128)(2,1)S(1)}, bf16[16,3,16,128]{3,2,1,0:T(8,128)(2,1)S(1)}, u32[]{:S(2)}, u32[]{:S(2)}) collective-permute-start(bf16[16,3,16,128]{3,2,1,0:T(8,128)(2,1)S(1)} %pad_maximum_fusion.3), channel_id=1, source_target_pairs={{0,16},{24,8},{16,32},{40,24},{32,48},{56,40},{48,49},{57,56},{49,... | collective-permute-start | bytes 589832 | tf_op jit(solution)/shard_map/ppermute | solution.py:385
  96.6 1.3 %collective-permute-start.11 = (bf16[16,16,128]{2,1,0:T(8,128)(2,1)S(1)}, bf16[16,16,128]{2,1,0:T(8,128)(2,1)S(1)}, u32[]{:S(2)}, u32[]{:S(2)}) collective-permute-start(bf16[16,16,128]{2,1,0:T(8,128)(2,1)S(1)} %dynamic-slice_bitcast_fusion), channel_id=1, source_target_pairs={{0,8},{8,0},{16,24},{24,16},{32,40},{40,32},{48,56},{56,48},{64,72... | collective-permute-start | bytes 196616 | tf_op jit(solution)/shard_map/ppermute | solution.py:386
  (16 other events, 48.1 us)

commit v3 on v2

--- a/solution.py
+++ b/solution.py
@@ -93,7 +93,6 @@
     last,
     tab,
     place,
-    own_f,
     own_b,
     part,
     side,
@@ -107,7 +106,6 @@
     wout,
     wskip,
     bout,
-    moved_f,
     moved_b,
     *rest,
 ):
@@ -152,24 +150,23 @@
         values = []
         for r in range(2):
             value = (
-                (0.9 - 0.05 * step) * own_f[src, r].astype(F32)
+                (0.9 - 0.05 * step) * own_b[src, r].astype(F32)
                 + acc[:, r * width : (r + 1) * width]
                 + 0.3 * noise[source, step - 1 if step else 1, q % 2, r].astype(F32)
             )
-            moved_f[t, r] = value
             moved_b[t, r] = value.astype(BF)
             values.append(value)
         if not last:
             rest[0][t, 0] = lax.select(low, values[1], values[0]).astype(BF)
 
     def body(t, carry):
-        normed = ready[...]
-        finish(jnp.maximum(t - 1, 0), normed)
-        following = convolve(t)
-        ready[...] = following
+        finish(t - 1, ready[...])
+        ready[...] = convolve(t)
         return carry
 
-    lax.fori_loop(0, tab[step, NUMBER] + 1, body, 0)
+    ready[...] = convolve(0)
+    lax.fori_loop(1, tab[step, NUMBER], body, 0)
+    finish(tab[step, NUMBER] - 1, ready[...])
     if last:
         final = rest[0]
 
@@ -181,8 +178,8 @@
 
 
 def run_step(step, last, *operands):
-    own_b, wconv = operands[3], operands[8]
-    outs = [jax.ShapeDtypeStruct(own_b.shape, F32), jax.ShapeDtypeStruct(own_b.shape, BF)]
+    own_b, wconv = operands[2], operands[7]
+    outs = [jax.ShapeDtypeStruct(own_b.shape, BF)]
     slots, each, channels, width = own_b.shape
     outs.append(jax.ShapeDtypeStruct((slots, each if last else 1, channels, width), BF))
     return pl.pallas_call(
@@ -310,28 +307,29 @@
 def spread_kernel(each, *refs):
     ins, out = refs[:-1], refs[-1]
     half = out.shape[0] // 2
+    channels = out.shape[4]
     rows = half * each
-    channels = out.shape[4]
-    images = [ref.at[a] for ref in ins for a in range(ref.shape[0])]
-    here = out.shape[2]
-    for n, image in enumerate(images):
-        for r in range(rows):
-            tile = image[pl.ds(r, channels, stride=rows), :].astype(BF)
-            for h in range(2):
-                out[h * half + r // each, n // here, n % here, r % each] = tile
-
-
-def spread_rows(parts, here, each, *arrays):
-    channels, rows, width = arrays[0].shape[1:]
-    images = sum(x.shape[0] for x in arrays)
+    for n, ref in enumerate(ins):
+        for j in range(ref.shape[0]):
+            for r in range(rows):
+                tile = ref[j, pl.ds(r, channels, stride=rows), :].astype(BF)
+                for h in range(2):
+                    out[h * half + r // each, n, j, r % each] = tile
+
+
+def spread_rows(parts, here, each, times, *arrays):
+    channels, rows, width = arrays[0][0].shape[1:]
+    block = (here, channels * rows, width)
+    out = (parts, len(arrays), here, each, channels, width)
     return pl.pallas_call(
         functools.partial(spread_kernel, each),
-        out_shape=jax.ShapeDtypeStruct((parts, images // here, here, each, channels, width), BF),
-        in_specs=[VMEM] * len(arrays),
-        out_specs=VMEM,
+        grid=(times,),
+        out_shape=jax.ShapeDtypeStruct((parts, times * len(arrays)) + out[2:], BF),
+        in_specs=[pl.BlockSpec(block, lambda i, at=at: (i + at, 0, 0)) for _, at in arrays],
+        out_specs=pl.BlockSpec(out, lambda i: (0, i, 0, 0, 0, 0)),
         compiler_params=pltpu.CompilerParams(vmem_limit_bytes=16 << 20),
         name="spread",
-    )(*[x.reshape(x.shape[0], channels * rows, width) for x in arrays])
+    )(*[pltpu.with_memory_space_constraint(x.reshape(x.shape[0], channels * rows, width), pltpu.HBM) for x, _ in arrays])
 
 
 def per_device(latent, ancestors, noise, embed, depth, depth_bias, gain, shift, inner, inner_bias, outer, outer_bias, head):
@@ -373,20 +371,18 @@
 
     flat = noise.reshape((-1,) + noise.shape[2:])
     params = weights(embed, depth, depth_bias, gain, shift, inner, inner_bias, outer, outer_bias, head, width)
-    first = spread_rows(parts, here, each, latent, flat[:here])
-    later = spread_rows(parts, here, each, flat[here:])
+    first = spread_rows(parts, here, each, 1, (latent, 0), (flat, 0))
+    later = spread_rows(parts, here, each, STEPS - 1, (flat, 1))
     first = deliver(first)
     later = deliver(later)
-    first, params = lax.optimization_barrier((first, params))
     own_b, near = pack(half * here, tab, place, first)
-    own_f = own_b
     for step in range(STEPS):
         part = lax.ppermute(own_b, "particle", swapped)
         side = lax.ppermute(jnp.concatenate([near, part], axis=1), both, sides)
         other = lax.ppermute(lax.dynamic_index_in_dim(side, 2 - core, axis=1, keepdims=False), "particle", swapped)
         drawn = first if step == 0 else later
-        outs = run_step(step, step == STEPS - 1, tab, place, own_f, own_b, part, side, other, drawn, *params)
-        own_f, own_b, near = outs
+        outs = run_step(step, step == STEPS - 1, tab, place, own_b, part, side, other, drawn, *params)
+        own_b, near = outs
     final = near.reshape(half, -1, width)
     home = lax.all_to_all(final, both, split_axis=0, concat_axis=0, axis_index_groups=halves, tiled=True)
     home = home.reshape(half, here, each, channels, width).transpose(1, 3, 0, 2, 4)

time: 119 us -> 118 us (level)
  the two profiles are of different devices: /device:TPU:22 before, /device:TPU:20 now
where the time goes in v3:
time: 118 us; the launch traced here: 117 us
  Pallas kernels  41.4 us (35%)
  waiting for transfers between devices  36.7 us (31%)
  starting transfers between devices  25.4 us (22%)
  blocking collectives  8.48 us (7%)
  local copies, waits for them, and re-layouts  3.64 us (3%)
  other arithmetic  1.52 us (1%)
    pallas_call x4, Pallas kernels, run_step(): pl.pallas_call(functools.partial(step_kernel, step, last), out_shape=outs...  28.8 us
    ppermute x4, waiting for transfers between devices, per_device(): side = lax.ppermute(jnp.concatenate([near, part], axis=1), both, sides)  24 us
    all_to_all x2, starting transfers between devices, deliver(): lax.all_to_all(x, both, split_axis=0, concat_axis=0, axis_index_groups=co...  14.9 us
    ppermute x4, starting transfers between devices, per_device(): side = lax.ppermute(jnp.concatenate([near, part], axis=1), both, sides)  9.81 us
    all_to_all x1, blocking collectives, per_device(): lax.all_to_all(final, both, split_axis=0, concat_axis=0, axis_index_group...  8.48 us
    ppermute x4, waiting for transfers between devices, per_device(): part = lax.ppermute(own_b, 'particle', swapped)  5.05 us
    pallas_call x2, Pallas kernels, spread_rows(): pl.pallas_call(functools.partial(spread_kernel, each), grid=(times,), out...  4.97 us
    pallas_call x1, Pallas kernels, make_table(): pl.pallas_call(functools.partial(table_kernel, final_count), out_shape=ja...  4.93 us
  transfers between devices with their start and end apart: 14, of which 12 were waited for; matrix products, arithmetic and copies ran while one was open for 1% of the time, Pallas kernels for 12%

profile of v3, /device:TPU:20, one launch (start us, length us, event | category | flops | bytes accessed | tf_op | source)
XLA Modules:
  0.0 117.4 jit_solution(13824476063962420696)
XLA Ops:
  0.0 2.0 %spread.2 = bf16[16,2,2,2,16,128]{5,4,3,2,1,0:T(8,128)(2,1)} custom-call(f32[2,256,128]{2,1,0:T(8,128)} %bitcast.44, f32[8,256,128]{2,1,0:T(8,128)} %bitcast.41), custom_call_target="tpu_custom_call" | custom-call | tf_op jit(solution)/shard_map/spread/pallas_call | solution.py:324
  2.0 8.3 %all-to-all-start = ((bf16[16,128,128]{2,1,0:T(8,128)(2,1)}), bf16[16,128,128]{2,1,0:T(8,128)(2,1)S(1)}, u32[]{:S(2)}, u32[]{:S(2)}) async-start(bf16[16,128,128]{2,1,0:T(8,128)(2,1)} %bitcast.5), calls=%async_computation | async-start | bytes 1048576 | tf_op jit(solution)/shard_map/all_to_all | solution.py:369
  10.9 4.9 %table.1.tab = s32[5,128]{1,0:T(8,128)} custom-call(s32[4,32]{1,0:T(4,128)} %anc.1, s32[3]{0:T(128)} %pad_add_fusion.place), custom_call_target="tpu_custom_call" | custom-call | tf_op jit(solution)/shard_map/table/pallas_call | solution.py:67
  15.8 3.9 %all-to-all-done = bf16[16,128,128]{2,1,0:T(8,128)(2,1)S(1)} async-done(((bf16[16,128,128]{2,1,0:T(8,128)(2,1)}), bf16[16,128,128]{2,1,0:T(8,128)(2,1)S(1)}, u32[]{:S(2)}, u32[]{:S(2)}) %all-to-all-start) | async-done | bytes 524320 | tf_op jit(solution)/shard_map/all_to_all | solution.py:369
  20.5 1.9 %pack.1 = (bf16[16,2,16,128]{3,2,1,0:T(8,128)(2,1)}, bf16[16,1,16,128]{3,2,1,0:T(8,128)(2,1)}) custom-call(s32[5,128]{1,0:T(8,128)} %table.1.tab, s32[3]{0:T(128)} %pad_add_fusion.place, bf16[16,2,2,2,16,128]{5,4,3,2,1,0:T(8,128)(2,1)} %bitcast.29), custom_call_target="tpu_custom_call" | custom-call | tf_op jit(solution)/shard_map/pack/pallas_call | solution.py:208
  22.6 1.4 %collective-permute-done.part = bf16[16,2,16,128]{3,2,1,0:T(8,128)(2,1)S(1)} collective-permute-done((bf16[16,2,16,128]{3,2,1,0:T(8,128)(2,1)}, bf16[16,2,16,128]{3,2,1,0:T(8,128)(2,1)S(1)}, u32[]{:S(2)}, u32[]{:S(2)}) %collective-permute-start) | collective-permute-done | bytes 131104 | tf_op jit(solution)/shard_map/ppermute | solution.py:380
  24.9 2.0 %collective-permute-start.1 = (bf16[16,3,16,128]{3,2,1,0:T(8,128)(2,1)S(1)}, bf16[16,3,16,128]{3,2,1,0:T(8,128)(2,1)S(1)}, u32[]{:S(2)}, u32[]{:S(2)}) collective-permute-start(bf16[16,3,16,128]{3,2,1,0:T(8,128)(2,1)S(1)} %pad_maximum_fusion), channel_id=1, source_target_pairs={{0,16},{24,8},{16,32},{40,24},{32,48},{56,40},{48,49},{57,56},{49,... | collective-permute-start | bytes 589832 | tf_op jit(solution)/shard_map/ppermute | solution.py:381
  26.9 6.4 %collective-permute-done.1.side = bf16[16,3,16,128]{3,2,1,0:T(8,128)(2,1)S(1)} collective-permute-done((bf16[16,3,16,128]{3,2,1,0:T(8,128)(2,1)S(1)}, bf16[16,3,16,128]{3,2,1,0:T(8,128)(2,1)S(1)}, u32[]{:S(2)}, u32[]{:S(2)}) %collective-permute-start.1) | collective-permute-done | bytes 196640 | tf_op jit(solution)/shard_map/ppermute | solution.py:381
  34.0 3.0 %spread.3 = bf16[16,3,2,2,16,128]{5,4,3,2,1,0:T(8,128)(2,1)} custom-call(f32[8,256,128]{2,1,0:T(8,128)} %bitcast.42), custom_call_target="tpu_custom_call" | custom-call | tf_op jit(solution)/shard_map/spread/pallas_call | solution.py:324
  37.0 6.6 %all-to-all-start.1 = ((bf16[16,192,128]{2,1,0:T(8,128)(2,1)}), bf16[16,192,128]{2,1,0:T(8,128)(2,1)S(1)}, u32[]{:S(2)}, u32[]{:S(2)}) async-start(bf16[16,192,128]{2,1,0:T(8,128)(2,1)} %bitcast.15), calls=%async_computation.1 | async-start | bytes 1572864 | tf_op jit(solution)/shard_map/all_to_all | solution.py:369
  45.8 5.0 %shard_map.127 = (bf16[16,2,16,128]{3,2,1,0:T(8,128)(2,1)S(1)}, bf16[16,1,16,128]{3,2,1,0:T(8,128)(2,1)S(1)}) custom-call(s32[5,128]{1,0:T(8,128)S(1)} %copy-done.5, s32[3]{0:T(128)S(1)} %copy-done.8, bf16[16,2,16,128]{3,2,1,0:T(8,128)(2,1)S(1)} %copy-done.16, bf16[16,2,16,128]{3,2,1,0:T(8,128)(2,1)S(1)} %collective-permute-done.part, ...), custom_call_target="tpu_custom_call" | custom-call | flops 4294967296 | bytes 4194304 | tf_op jit(solution)/shard_map/pallas_call | solution.py:185
  52.3 3.4 %collective-permute-start.4 = (bf16[16,3,16,128]{3,2,1,0:T(8,128)(2,1)S(1)}, bf16[16,3,16,128]{3,2,1,0:T(8,128)(2,1)S(1)}, u32[]{:S(2)}, u32[]{:S(2)}) collective-permute-start(bf16[16,3,16,128]{3,2,1,0:T(8,128)(2,1)S(1)} %pad_maximum_fusion.1), channel_id=1, source_target_pairs={{0,16},{24,8},{16,32},{40,24},{32,48},{56,40},{48,49},{57,56},{49,... | collective-permute-start | bytes 589832 | tf_op jit(solution)/shard_map/ppermute | solution.py:381
  55.7 5.1 %collective-permute-done.4.side = bf16[16,3,16,128]{3,2,1,0:T(8,128)(2,1)S(1)} collective-permute-done((bf16[16,3,16,128]{3,2,1,0:T(8,128)(2,1)S(1)}, bf16[16,3,16,128]{3,2,1,0:T(8,128)(2,1)S(1)}, u32[]{:S(2)}, u32[]{:S(2)}) %collective-permute-start.4) | collective-permute-done | bytes 196640 | tf_op jit(solution)/shard_map/ppermute | solution.py:381
  60.8 1.2 %collective-permute-done.5.other = bf16[16,16,128]{2,1,0:T(8,128)(2,1)S(1)} collective-permute-done((bf16[16,16,128]{2,1,0:T(8,128)(2,1)S(1)}, bf16[16,16,128]{2,1,0:T(8,128)(2,1)S(1)}, u32[]{:S(2)}, u32[]{:S(2)}) %collective-permute-start.5) | collective-permute-done | bytes 65568 | tf_op jit(solution)/shard_map/ppermute | solution.py:382
  62.0 5.5 %shard_map.128 = (bf16[16,2,16,128]{3,2,1,0:T(8,128)(2,1)S(1)}, bf16[16,1,16,128]{3,2,1,0:T(8,128)(2,1)S(1)}) custom-call(s32[5,128]{1,0:T(8,128)S(1)} %copy-done.5, s32[3]{0:T(128)S(1)} %copy-done.8, bf16[16,2,16,128]{3,2,1,0:T(8,128)(2,1)S(1)} %get-tuple-element.32.own_b, bf16[16,2,16,128]{3,2,1,0:T(8,128)(2,1)S(1)} %collective-permute-done.3.part, ...), custom_call_target="tpu_custom_call" | custom-call | flops 4294967296 | bytes 4194304 | tf_op jit(solution)/shard_map/pallas_call | solution.py:185
  68.9 2.5 %collective-permute-start.7 = (bf16[16,3,16,128]{3,2,1,0:T(8,128)(2,1)S(1)}, bf16[16,3,16,128]{3,2,1,0:T(8,128)(2,1)S(1)}, u32[]{:S(2)}, u32[]{:S(2)}) collective-permute-start(bf16[16,3,16,128]{3,2,1,0:T(8,128)(2,1)S(1)} %pad_maximum_fusion.2), channel_id=1, source_target_pairs={{0,16},{24,8},{16,32},{40,24},{32,48},{56,40},{48,49},{57,56},{49,... | collective-permute-start | bytes 589832 | tf_op jit(solution)/shard_map/ppermute | solution.py:381
  71.4 6.0 %collective-permute-done.7.side = bf16[16,3,16,128]{3,2,1,0:T(8,128)(2,1)S(1)} collective-permute-done((bf16[16,3,16,128]{3,2,1,0:T(8,128)(2,1)S(1)}, bf16[16,3,16,128]{3,2,1,0:T(8,128)(2,1)S(1)}, u32[]{:S(2)}, u32[]{:S(2)}) %collective-permute-start.7) | collective-permute-done | bytes 196640 | tf_op jit(solution)/shard_map/ppermute | solution.py:381
  77.3 1.2 %collective-permute-done.8.other = bf16[16,16,128]{2,1,0:T(8,128)(2,1)S(1)} collective-permute-done((bf16[16,16,128]{2,1,0:T(8,128)(2,1)S(1)}, bf16[16,16,128]{2,1,0:T(8,128)(2,1)S(1)}, u32[]{:S(2)}, u32[]{:S(2)}) %collective-permute-start.8) | collective-permute-done | bytes 65568 | tf_op jit(solution)/shard_map/ppermute | solution.py:382
  78.6 7.7 %shard_map.129 = (bf16[16,2,16,128]{3,2,1,0:T(8,128)(2,1)S(1)}, bf16[16,1,16,128]{3,2,1,0:T(8,128)(2,1)S(1)}) custom-call(s32[5,128]{1,0:T(8,128)S(1)} %copy-done.5, s32[3]{0:T(128)S(1)} %copy-done.8, bf16[16,2,16,128]{3,2,1,0:T(8,128)(2,1)S(1)} %get-tuple-element.34.own_b, bf16[16,2,16,128]{3,2,1,0:T(8,128)(2,1)S(1)} %collective-permute-done.6.part, ...), custom_call_target="tpu_custom_call" | custom-call | flops 4294967296 | bytes 4194304 | tf_op jit(solution)/shard_map/pallas_call | solution.py:185
  87.7 1.9 %collective-permute-start.10 = (bf16[16,3,16,128]{3,2,1,0:T(8,128)(2,1)S(1)}, bf16[16,3,16,128]{3,2,1,0:T(8,128)(2,1)S(1)}, u32[]{:S(2)}, u32[]{:S(2)}) collective-permute-start(bf16[16,3,16,128]{3,2,1,0:T(8,128)(2,1)S(1)} %pad_maximum_fusion.3), channel_id=1, source_target_pairs={{0,16},{24,8},{16,32},{40,24},{32,48},{56,40},{48,49},{57,56},{49,... | collective-permute-start | bytes 589832 | tf_op jit(solution)/shard_map/ppermute | solution.py:381
  89.6 6.5 %collective-permute-done.10.side = bf16[16,3,16,128]{3,2,1,0:T(8,128)(2,1)S(1)} collective-permute-done((bf16[16,3,16,128]{3,2,1,0:T(8,128)(2,1)S(1)}, bf16[16,3,16,128]{3,2,1,0:T(8,128)(2,1)S(1)}, u32[]{:S(2)}, u32[]{:S(2)}) %collective-permute-start.10) | collective-permute-done | bytes 196640 | tf_op jit(solution)/shard_map/ppermute | solution.py:381
  96.2 1.2 %collective-permute-done.11.other = bf16[16,16,128]{2,1,0:T(8,128)(2,1)S(1)} collective-permute-done((bf16[16,16,128]{2,1,0:T(8,128)(2,1)S(1)}, bf16[16,16,128]{2,1,0:T(8,128)(2,1)S(1)}, u32[]{:S(2)}, u32[]{:S(2)}) %collective-permute-start.11) | collective-permute-done | bytes 65568 | tf_op jit(solution)/shard_map/ppermute | solution.py:382
  97.4 10.7 %shard_map.130 = (bf16[16,2,16,128]{3,2,1,0:T(8,128)(2,1)}, bf16[16,2,16,128]{3,2,1,0:T(8,128)(2,1)S(1)}) custom-call(s32[5,128]{1,0:T(8,128)S(1)} %copy-done.5, s32[3]{0:T(128)S(1)} %copy-done.8, bf16[16,2,16,128]{3,2,1,0:T(8,128)(2,1)S(1)} %get-tuple-element.36.own_b, bf16[16,2,16,128]{3,2,1,0:T(8,128)(2,1)S(1)} %collective-permute-done.9.part, ...), custom_call_target="tpu_custom_call" | custom-call | flops 4294967296 | bytes 4194304 | tf_op jit(solution)/shard_map/pallas_call | solution.py:185
  108.1 8.5 %all_to_all.15 = bf16[8,64,128]{2,1,0:T(8,128)(2,1)S(1)} all-to-all(bf16[8,64,128]{2,1,0:T(8,128)(2,1)S(1)} %bitcast.34), channel_id=1, replica_groups={{0,8,16,24,32,40,48,56},{64,72,80,88,96,104,112,120},{49,57,33,41,17,25..., dimensions={0} | all-to-all | bytes 262144 | tf_op jit(solution)/shard_map/all_to_all | solution.py:387
  (62 shorter events, 10.1 us)
Async XLA Ops:
  2.0 17.8 %all-to-all-start = ((bf16[16,128,128]{2,1,0:T(8,128)(2,1)}), bf16[16,128,128]{2,1,0:T(8,128)(2,1)S(1)}, u32[]{:S(2)}, u32[]{:S(2)}) async-start(bf16[16,128,128]{2,1,0:T(8,128)(2,1)} %bitcast.5), calls=%async_computation | async-start | bytes 1048576 | tf_op jit(solution)/shard_map/all_to_all | solution.py:369
  22.5 1.6 %collective-permute-start = (bf16[16,2,16,128]{3,2,1,0:T(8,128)(2,1)}, bf16[16,2,16,128]{3,2,1,0:T(8,128)(2,1)S(1)}, u32[]{:S(2)}, u32[]{:S(2)}) collective-permute-start(bf16[16,2,16,128]{3,2,1,0:T(8,128)(2,1)} %get-tuple-element.22.own_b), channel_id=1, source_target_pairs={{0,8},{8,0},{16,24},{24,16},{32,40},{40,32},{48,56},{56,48},{64,72... | collective-permute-start | bytes 393224 | tf_op jit(solution)/shard_map/ppermute | solution.py:380
  24.9 8.5 %collective-permute-start.1 = (bf16[16,3,16,128]{3,2,1,0:T(8,128)(2,1)S(1)}, bf16[16,3,16,128]{3,2,1,0:T(8,128)(2,1)S(1)}, u32[]{:S(2)}, u32[]{:S(2)}) collective-permute-start(bf16[16,3,16,128]{3,2,1,0:T(8,128)(2,1)S(1)} %pad_maximum_fusion), channel_id=1, source_target_pairs={{0,16},{24,8},{16,32},{40,24},{32,48},{56,40},{48,49},{57,56},{49,... | collective-permute-start | bytes 589832 | tf_op jit(solution)/shard_map/ppermute | solution.py:381
  34.0 11.0 %collective-permute-start.2 = (bf16[16,16,128]{2,1,0:T(8,128)(2,1)}, bf16[16,16,128]{2,1,0:T(8,128)(2,1)}, u32[]{:S(2)}, u32[]{:S(2)}) collective-permute-start(bf16[16,16,128]{2,1,0:T(8,128)(2,1)} %dynamic-slice_bitcast_fusion.3), channel_id=1, source_target_pairs={{0,8},{8,0},{16,24},{24,16},{32,40},{40,32},{48,56},{56,48},{64,72... | collective-permute-start | bytes 196616 | tf_op jit(solution)/shard_map/ppermute | solution.py:382
  37.0 6.6 %copy-start.2 = (bf16[256,1024]{1,0:T(8,128)(2,1)S(1)}, bf16[256,1024]{1,0:T(8,128)(2,1)}, u32[]{:S(2)}) copy-start(bf16[256,1024]{1,0:T(8,128)(2,1)} %inner.1) | copy-start | bytes 1572868
  37.0 6.7 %copy-start.3 = (bf16[1024,256]{1,0:T(8,128)(2,1)S(1)}, bf16[1024,256]{1,0:T(8,128)(2,1)}, u32[]{:S(2)}) copy-start(bf16[1024,256]{1,0:T(8,128)(2,1)} %outer.1) | copy-start | bytes 1572868
  37.0 6.7 %copy-start.4 = (bf16[7,7,256]{2,1,0:T(8,128)(2,1)S(1)}, bf16[7,7,256]{2,1,0:T(8,128)(2,1)}, u32[]{:S(2)}) copy-start(bf16[7,7,256]{2,1,0:T(8,128)(2,1)} %depth.1) | copy-start | bytes 75268
  37.0 6.7 %copy-start.7 = (bf16[256,16]{0,1:T(8,128)(2,1)S(1)}, bf16[256,16]{0,1:T(8,128)(2,1)}, u32[]{:S(2)}) copy-start(bf16[256,16]{0,1:T(8,128)(2,1)} %param.25) | copy-start | bytes 24580
  37.0 6.7 %copy-start.9 = (f32[1024]{0:T(1024)S(1)}, f32[1024]{0:T(1024)}, u32[]{:S(2)}) copy-start(f32[1024]{0:T(1024)} %param.22) | copy-start | bytes 12292
  37.0 6.7 %copy-start.11 = (f32[256]{0:T(256)S(1)}, f32[256]{0:T(256)}, u32[]{:S(2)}) copy-start(f32[256]{0:T(256)} %param.19) | copy-start | bytes 3076
  37.0 6.7 %copy-start.12 = (f32[256]{0:T(256)S(1)}, f32[256]{0:T(256)}, u32[]{:S(2)}) copy-start(f32[256]{0:T(256)} %param.20) | copy-start | bytes 3076
  37.0 6.7 %copy-start.13 = (f32[256]{0:T(256)S(1)}, f32[256]{0:T(256)}, u32[]{:S(2)}) copy-start(f32[256]{0:T(256)} %param.24) | copy-start | bytes 3076
  37.0 23.7 %all-to-all-start.1 = ((bf16[16,192,128]{2,1,0:T(8,128)(2,1)}), bf16[16,192,128]{2,1,0:T(8,128)(2,1)S(1)}, u32[]{:S(2)}, u32[]{:S(2)}) async-start(bf16[16,192,128]{2,1,0:T(8,128)(2,1)} %bitcast.15), calls=%async_computation.1 | async-start | bytes 1572864 | tf_op jit(solution)/shard_map/all_to_all | solution.py:369
  50.8 11.2 %copy-start.15 = (bf16[256,800]{1,0:T(8,128)(2,1)S(1)}, bf16[256,800]{1,0:T(8,128)(2,1)}, u32[]{:S(2)}) copy-start(bf16[256,800]{1,0:T(8,128)(2,1)} %copy-done.14) | copy-start | bytes 1228804
  50.8 1.4 %collective-permute-start.3 = (bf16[16,2,16,128]{3,2,1,0:T(8,128)(2,1)S(1)}, bf16[16,2,16,128]{3,2,1,0:T(8,128)(2,1)S(1)}, u32[]{:S(2)}, u32[]{:S(2)}) collective-permute-start(bf16[16,2,16,128]{3,2,1,0:T(8,128)(2,1)S(1)} %get-tuple-element.32.own_b), channel_id=1, source_target_pairs={{0,8},{8,0},{16,24},{24,16},{32,40},{40,32},{48,56},{56,48},{64,72... | collective-permute-start | bytes 393224 | tf_op jit(solution)/shard_map/ppermute | solution.py:380
  52.3 9.7 %copy-start.18 = (bf16[16,1024]{1,0:T(8,128)(2,1)S(1)}, bf16[16,1024]{1,0:T(8,128)(2,1)}, u32[]{:S(2)}) copy-start(bf16[16,1024]{1,0:T(8,128)(2,1)} %copy-done.17) | copy-start | bytes 98308
  52.3 8.5 %collective-permute-start.4 = (bf16[16,3,16,128]{3,2,1,0:T(8,128)(2,1)S(1)}, bf16[16,3,16,128]{3,2,1,0:T(8,128)(2,1)S(1)}, u32[]{:S(2)}, u32[]{:S(2)}) collective-permute-start(bf16[16,3,16,128]{3,2,1,0:T(8,128)(2,1)S(1)} %pad_maximum_fusion.1), channel_id=1, source_target_pairs={{0,16},{24,8},{16,32},{40,24},{32,48},{56,40},{48,49},{57,56},{49,... | collective-permute-start | bytes 589832 | tf_op jit(solution)/shard_map/ppermute | solution.py:381
  60.7 1.3 %collective-permute-start.5 = (bf16[16,16,128]{2,1,0:T(8,128)(2,1)S(1)}, bf16[16,16,128]{2,1,0:T(8,128)(2,1)S(1)}, u32[]{:S(2)}, u32[]{:S(2)}) collective-permute-start(bf16[16,16,128]{2,1,0:T(8,128)(2,1)S(1)} %dynamic-slice_bitcast_fusion.2), channel_id=1, source_target_pairs={{0,8},{8,0},{16,24},{24,16},{32,40},{40,32},{48,56},{56,48},{64,72... | collective-permute-start | bytes 196616 | tf_op jit(solution)/shard_map/ppermute | solution.py:382
  67.5 1.4 %collective-permute-start.6 = (bf16[16,2,16,128]{3,2,1,0:T(8,128)(2,1)S(1)}, bf16[16,2,16,128]{3,2,1,0:T(8,128)(2,1)S(1)}, u32[]{:S(2)}, u32[]{:S(2)}) collective-permute-start(bf16[16,2,16,128]{3,2,1,0:T(8,128)(2,1)S(1)} %get-tuple-element.34.own_b), channel_id=1, source_target_pairs={{0,8},{8,0},{16,24},{24,16},{32,40},{40,32},{48,56},{56,48},{64,72... | collective-permute-start | bytes 393224 | tf_op jit(solution)/shard_map/ppermute | solution.py:380
  68.9 8.5 %collective-permute-start.7 = (bf16[16,3,16,128]{3,2,1,0:T(8,128)(2,1)S(1)}, bf16[16,3,16,128]{3,2,1,0:T(8,128)(2,1)S(1)}, u32[]{:S(2)}, u32[]{:S(2)}) collective-permute-start(bf16[16,3,16,128]{3,2,1,0:T(8,128)(2,1)S(1)} %pad_maximum_fusion.2), channel_id=1, source_target_pairs={{0,16},{24,8},{16,32},{40,24},{32,48},{56,40},{48,49},{57,56},{49,... | collective-permute-start | bytes 589832 | tf_op jit(solution)/shard_map/ppermute | solution.py:381
  77.3 1.3 %collective-permute-start.8 = (bf16[16,16,128]{2,1,0:T(8,128)(2,1)S(1)}, bf16[16,16,128]{2,1,0:T(8,128)(2,1)S(1)}, u32[]{:S(2)}, u32[]{:S(2)}) collective-permute-start(bf16[16,16,128]{2,1,0:T(8,128)(2,1)S(1)} %dynamic-slice_bitcast_fusion.1), channel_id=1, source_target_pairs={{0,8},{8,0},{16,24},{24,16},{32,40},{40,32},{48,56},{56,48},{64,72... | collective-permute-start | bytes 196616 | tf_op jit(solution)/shard_map/ppermute | solution.py:382
  86.3 1.4 %collective-permute-start.9 = (bf16[16,2,16,128]{3,2,1,0:T(8,128)(2,1)S(1)}, bf16[16,2,16,128]{3,2,1,0:T(8,128)(2,1)S(1)}, u32[]{:S(2)}, u32[]{:S(2)}) collective-permute-start(bf16[16,2,16,128]{3,2,1,0:T(8,128)(2,1)S(1)} %get-tuple-element.36.own_b), channel_id=1, source_target_pairs={{0,8},{8,0},{16,24},{24,16},{32,40},{40,32},{48,56},{56,48},{64,72... | collective-permute-start | bytes 393224 | tf_op jit(solution)/shard_map/ppermute | solution.py:380
  87.7 8.5 %collective-permute-start.10 = (bf16[16,3,16,128]{3,2,1,0:T(8,128)(2,1)S(1)}, bf16[16,3,16,128]{3,2,1,0:T(8,128)(2,1)S(1)}, u32[]{:S(2)}, u32[]{:S(2)}) collective-permute-start(bf16[16,3,16,128]{3,2,1,0:T(8,128)(2,1)S(1)} %pad_maximum_fusion.3), channel_id=1, source_target_pairs={{0,16},{24,8},{16,32},{40,24},{32,48},{56,40},{48,49},{57,56},{49,... | collective-permute-start | bytes 589832 | tf_op jit(solution)/shard_map/ppermute | solution.py:381
  96.2 1.3 %collective-permute-start.11 = (bf16[16,16,128]{2,1,0:T(8,128)(2,1)S(1)}, bf16[16,16,128]{2,1,0:T(8,128)(2,1)S(1)}, u32[]{:S(2)}, u32[]{:S(2)}) collective-permute-start(bf16[16,16,128]{2,1,0:T(8,128)(2,1)S(1)} %dynamic-slice_bitcast_fusion), channel_id=1, source_target_pairs={{0,8},{8,0},{16,24},{24,16},{32,40},{40,32},{48,56},{56,48},{64,72... | collective-permute-start | bytes 196616 | tf_op jit(solution)/shard_map/ppermute | solution.py:382
  (9 other events, 17.3 us)
